TPU v7x, 128 devices: a whole 4x4x4 slice. The times are simulated.
128 devices in a mesh: group: 4 (over y_lo, core), mp: 32 (over z, x, y_hi).
Axes of the slice: x: 4, y: 4 (y_hi: 2, y_lo: 2; y = y_hi * 2 + y_lo), z: 4, core: 2. Of those that a mesh axis runs over, the one named last changes fastest.
Arguments:
- tokens: bfloat16 [5120, 2048], P(('group', 'mp')), may hold values from -6 to 6
- lengths: int32 [4, 8], P('group'), may hold values from 1 to 512, 1280 in all within a row
- query_gain: float32 [2048], replicated, may hold values from 0.5 to 8
- key_gain: float32 [2048], replicated, may hold values from 0.5 to 8
- attn_post_gain: float32 [2048], replicated, may hold values from 0.5 to 1.5
- mlp_post_gain: float32 [2048], replicated, may hold values from 0.5 to 1.5
- query_weight: float32 [2048, 2048], P(('mp', 'group')), may hold values from -4 to 4
- key_weight: float32 [2048, 2048], P(('mp', 'group')), may hold values from -4 to 4
- value_weight: float32 [2048, 2048], P(('mp', 'group')), may hold values from -0.125 to 0.125
- output_weight: float32 [2048, 2048], P(('mp', 'group')), may hold values from -0.125 to 0.125
- gate_weight: float32 [2048, 8192], P(('mp', 'group')), may hold values from -0.125 to 0.125
- up_weight: float32 [2048, 8192], P(('mp', 'group')), may hold values from -0.125 to 0.125
- down_weight: float32 [8192, 2048], P(('mp', 'group')), may hold values from -0.0625 to 0.0625
Outputs:
- layer_out: bfloat16 [5120, 2048], P(('group', 'mp'))
Inputs may be any that keep to these rules, and one draw needn't show every extreme that they name: In each group the 8 prompt lengths sum to 1280; the longest is exactly 512.
All inputs are finite; a program needn't handle non-finite values.
Results may differ from a plain program's by a relative error of at most 0.034.
Values may be sent and summed in bfloat16 or wider, within the bound.
A program may use at most 64 MiB of HBM per device.

v0:
```python
import math

import jax
import jax.numpy as jnp
from jax import lax
from jax.sharding import PartitionSpec as P

HEAD_DIM = 128


NORM_EPSILON = 1e-06
ROPE_BASE = 500000.0


def partner_2(block, axis, apart):
    count = lax.axis_size(axis)
    route = []
    for low in range(count):
        high = low | 1 << apart
        if high != low and high < count:
            route += [(low, high), (high, low)]
    return lax.ppermute(block, axis, route)


def token_layout(prompt_lens, row_count):
    seg_ends = jnp.cumsum(prompt_lens)
    starts = seg_ends - prompt_lens
    indices = jnp.arange(row_count, dtype=jnp.int32)
    segment = jnp.sum((indices[:, None] >= seg_ends[None, :]).astype(jnp.int32), axis=1)
    member = segment[:, None] == jnp.arange(prompt_lens.shape[0], dtype=jnp.int32)[None, :]
    opening = jnp.sum(jnp.where(member, starts[None, :], 0), axis=1)
    return (segment, indices - opening)


def rotary(head_values, position, head_size):
    half_size = head_size // 2
    frequency = jnp.exp(
        jnp.arange(half_size, dtype=jnp.float32) * (-2.0 * math.log(ROPE_BASE) / head_size)
    )
    angles = position.astype(jnp.float32)[:, None] * frequency[None, :]
    cosines = jnp.cos(angles)
    sines = jnp.sin(angles)
    front_half = head_values[..., :half_size]
    back_half = head_values[..., half_size:]
    return jnp.concatenate(
        [front_half * cosines - back_half * sines, back_half * cosines + front_half * sines],
        axis=-1,
    )


def head_attention(queries, query_rows, keys_rot, values_h, segment, head_size):
    scores = lax.dot_general(
        queries, keys_rot, (((1,), (1,)), ((), ())), preferred_element_type=jnp.float32
    )
    scores = scores * (1.0 / math.sqrt(head_size))
    key_rows = jnp.arange(keys_rot.shape[0], dtype=jnp.int32)
    query_segment = jnp.take(segment, query_rows)
    allowed = (query_segment[:, None] == segment[None, :]) & (
        key_rows[None, :] <= query_rows[:, None]
    )
    scores = jnp.where(allowed, scores, -1e30)
    row_max = jnp.max(scores, axis=1, keepdims=True)
    weights = jnp.exp(scores - row_max)
    weights = weights / jnp.sum(weights, axis=1, keepdims=True)
    probabilities = weights.astype(jnp.bfloat16)
    return jnp.dot(probabilities, values_h, preferred_element_type=jnp.float32).astype(jnp.bfloat16)


def rms_scale(values_in, gain):
    return (
        values_in
        * lax.rsqrt(jnp.mean(values_in * values_in, axis=-1, keepdims=True) + NORM_EPSILON)
        * gain
    )


def per_device(
    tokens,
    lengths,
    query_gain,
    key_gain,
    attn_post_gain,
    mlp_post_gain,
    query_weight,
    key_weight,
    value_weight,
    output_weight,
    gate_weight,
    up_weight,
    down_weight,
):
    features = tokens.shape[1]
    shards = lax.axis_size("mp")
    my_index = lax.axis_index("mp")
    col_width = features // shards
    tok_rows = tokens.shape[0]
    group_rows = tok_rows * shards
    stack_attn = jnp.stack([query_weight, key_weight, value_weight]).astype(jnp.bfloat16)
    stack_mlp = jnp.stack([gate_weight, up_weight]).astype(jnp.bfloat16)
    down_piece = down_weight.astype(jnp.bfloat16)[None]
    output_piece = output_weight.astype(jnp.bfloat16)[None]
    attn_rows, mlp_rows, down_rows, output_rows = (
        lax.all_gather(stack_attn, "group", axis=1, tiled=True),
        lax.all_gather(stack_mlp, "group", axis=1, tiled=True),
        lax.all_gather(down_piece, "group", axis=1, tiled=True),
        lax.all_gather(output_piece, "group", axis=1, tiled=True),
    )
    attn_block, mlp_block = (
        lax.all_to_all(attn_rows, "mp", split_axis=2, concat_axis=1, tiled=True),
        lax.all_to_all(mlp_rows, "mp", split_axis=2, concat_axis=1, tiled=True),
    )
    down_block = down_rows[0]
    output_block = output_rows[0]
    parity = my_index % 2
    partner = partner_2(attn_block, "mp", 0)
    attn_block = jnp.where(
        parity == 0,
        jnp.concatenate([attn_block, partner], axis=2),
        jnp.concatenate([partner, attn_block], axis=2),
    )
    head_cols = attn_block.shape[2]
    col_start = my_index * col_width // HEAD_DIM * HEAD_DIM
    share_part = col_width / head_cols
    projected = jnp.einsum(
        "td,kdc->ktc",
        lax.all_gather(tokens, "mp", axis=0, tiled=True),
        attn_block,
        preferred_element_type=jnp.float32,
    )
    query_sq = jnp.sum(projected[0] * projected[0], axis=1) * share_part
    key_sq = jnp.sum(projected[1] * projected[1], axis=1) * share_part
    query_total, key_total = lax.psum((query_sq, key_sq), "mp")
    query_part = lax.dynamic_slice_in_dim(query_gain, col_start, head_cols)
    key_part = lax.dynamic_slice_in_dim(key_gain, col_start, head_cols)
    q_normed = projected[0] * lax.rsqrt(query_total / features + NORM_EPSILON)[:, None] * query_part
    k_normed = projected[1] * lax.rsqrt(key_total / features + NORM_EPSILON)[:, None] * key_part
    segment, position = token_layout(lengths[0], group_rows)
    local_heads = head_cols // HEAD_DIM

    def heads_first(flat):
        return flat.reshape(group_rows, local_heads, HEAD_DIM).transpose(1, 0, 2)

    queries = rotary(heads_first(q_normed), position, HEAD_DIM).astype(jnp.bfloat16)
    keys_rot = rotary(heads_first(k_normed), position, HEAD_DIM).astype(jnp.bfloat16)
    values_h = heads_first(projected[2].astype(jnp.bfloat16))
    all_rows = jnp.arange(group_rows, dtype=jnp.int32)

    def per_head(triple):
        return head_attention(triple[0], all_rows, triple[1], triple[2], segment, HEAD_DIM)

    attended = lax.map(per_head, (queries, keys_rot, values_h))
    attended = attended.transpose(1, 0, 2).reshape(group_rows, head_cols)
    attended = lax.dynamic_slice_in_dim(attended, parity * col_width, col_width, 1)
    rows_part = attended
    attn_out = lax.psum_scatter(
        jnp.dot(rows_part, output_block, preferred_element_type=jnp.float32).astype(jnp.bfloat16),
        "mp",
        scatter_dimension=0,
        tiled=True,
    ).astype(jnp.float32)
    hidden = (tokens.astype(jnp.float32) + rms_scale(attn_out, attn_post_gain)).astype(jnp.bfloat16)
    hidden_width = mlp_block.shape[2]
    mlp_weights = jnp.concatenate([mlp_block[0], mlp_block[1]], axis=1)
    both_proj = jnp.dot(
        lax.all_gather(hidden, "mp", axis=0, tiled=True),
        mlp_weights,
        preferred_element_type=jnp.float32,
    )
    activated = (jax.nn.silu(both_proj[:, :hidden_width]) * both_proj[:, hidden_width:]).astype(
        jnp.bfloat16
    )
    rows_part = activated
    mlp_out = lax.psum_scatter(
        jnp.dot(rows_part, down_block, preferred_element_type=jnp.float32).astype(jnp.bfloat16),
        "mp",
        scatter_dimension=0,
        tiled=True,
    ).astype(jnp.float32)
    return (hidden.astype(jnp.float32) + rms_scale(mlp_out, mlp_post_gain)).astype(jnp.bfloat16)


def solution(mesh):
    return jax.shard_map(
        per_device,
        mesh=mesh,
        in_specs=(
            P(("group", "mp"), None),
            P("group", None),
            P(),
            P(),
            P(),
            P(),
            P(("mp", "group"), None),
            P(("mp", "group"), None),
            P(("mp", "group"), None),
            P(("mp", "group"), None),
            P(("mp", "group"), None),
            P(("mp", "group"), None),
            P(("mp", "group"), None),
        ),
        out_specs=P(("group", "mp"), None),
        check_vma=False,
    )
```

profile of v0, /device:TPU:0, one launch (start us, length us, event | category | flops | bytes accessed | tf_op | source)
XLA Modules:
  0.0 826.0 jit_solution(16544474879725775960)
XLA Ops:
  7.4 0.7 all-gather.7.cloned.1.call-update
  8.1 0.9 convert_bitcast_fusion.4
  9.0 1.0 convert_bitcast_fusion.2
  10.0 8.8 %all_gather.18 = bf16[3,64,2048]{2,1,0:T(8,128)(2,1)S(1)} all-gather(bf16[3,16,2048]{2,1,0:T(8,128)(2,1)S(1)} %pad_maximum_fusion.1), channel_id=1, replica_groups=mesh['group'=4,'mp'=32] {'group'}, dimensions={1}, use_global_device_ids=true | all-gather | bytes 983040 | tf_op jit(solution)/shard_map/all_gather | solution.py:103
  18.8 1.4 copy.34
  20.2 2.5 reshape.221
  22.6 10.5 %all-to-all-start = ((bf16[32,2,6144]{2,1,0:T(2,128)(2,1)}), bf16[32,2,6144]{2,1,0:T(2,128)(2,1)S(1)}, u32[]{:S(2)}, u32[]{:S(2)}) async-start(bf16[32,2,6144]{2,1,0:T(2,128)(2,1)} %reshape.221), calls=%async_computation | async-start | bytes 1572864 | tf_op jit(solution)/shard_map/all_to_all | solution.py:109
  33.1 0.0 reduce-scatter.3.cloned.1.call-start
  33.2 0.8 dynamic_slice.16
  34.0 0.8 dynamic_slice.17
  34.7 0.2 reduce-window.4
  35.0 0.1 convert_reduce_fusion
  35.0 7.1 gather_fusion
  42.1 5.8 all-gather
  47.9 2.3 all-to-all-done
  50.3 1.3 reshape.222
  51.6 2.5 copy.35
  54.1 2.8 all_to_all.27
  56.9 1.0 collective-permute-start
  57.9 0.1 select_reduce_fusion
  58.0 20.9 %collective-permute-done = bf16[3,2048,64]{1,2,0:T(8,128)(2,1)S(1)} collective-permute-done((bf16[3,2048,64]{1,2,0:T(8,128)(2,1)S(1)}, bf16[3,2048,64]{1,2,0:T(8,128)(2,1)S(1)}, u32[]{:S(2)}, u32[]{:S(2)}) %collective-permute-start) | collective-permute-done | bytes 786464 | tf_op jit(solution)/shard_map/ppermute | solution.py:22
  78.9 0.9 copy-done.8
  79.9 24.5 %all-gather.7.cloned.1.call-done = bf16[1280,2048]{1,0:T(8,128)(2,1)} async-done(((bf16[40,2048]{1,0:T(8,128)(2,1)}), bf16[1280,2048]{1,0:T(8,128)(2,1)}) %all-gather.7.cloned.1.call-update) | async-done | bytes 5242896 | tf_op jit(solution)/shard_map/all_gather | solution.py:126
  104.3 5.2 fusion.6
  109.6 0.1 multiply_reduce_fusion
  109.7 181.7 %all-reduce = (f32[1280]{0:T(1024)S(1)}, f32[1280]{0:T(1024)S(1)}) all-reduce(f32[1280]{0:T(1024)S(1)} %broadcast_multiply_fusion.1, f32[1280]{0:T(1024)S(1)} %broadcast_multiply_fusion), channel_id=1, replica_groups=mesh['group'=4,'mp'=32] {'mp'}, use_global_device_ids=true, to_apply=%region_3.4 | all-reduce | flops 2560 | bytes 20480 | tf_op jit(solution)/shard_map/psum | solution.py:132
  291.4 0.2 multiply_multiply_fusion
  291.6 1.5 fusion.55
  293.1 1.5 fusion.66
  294.6 1.0 fusion.2
  295.6 1.3 fusion.5
  296.9 3.9 convolution_convert_fusion.1
  300.8 0.0 all-gather.11.cloned.1.call-start
  300.9 1.0 copy-done.2
  301.8 0.2 copy-done.3
  302.0 0.1 convert_bitcast_fusion
  302.0 0.9 pad_maximum_fusion
  302.9 0.0 all-gather.11.cloned.1.call-update
  302.9 0.0 all-gather.9.cloned.1.call-start
  303.0 195.8 %reduce-scatter.3.cloned.1.call-done = bf16[40,2048]{1,0:T(8,128)(2,1)} async-done(((bf16[1280,2048]{1,0:T(8,128)(2,1)}), bf16[40,2048]{1,0:T(8,128)(2,1)}) %reduce-scatter.3.cloned.1.call-update) | async-done | bytes 163856 | tf_op jit(solution)/shard_map/reduce_scatter | solution.py:155
  498.7 1.1 fusion.30
  499.8 1.7 fusion.33
  501.5 0.0 all-gather.11.cloned.1.call-done
  501.6 9.6 %copy.36 = bf16[2,64,8192]{1,0,2:T(2,128)(2,1)} copy(bf16[2,64,8192]{2,1,0:T(8,128)(2,1)} %all-gather.11.cloned.1.call-done) | data formatting | bytes 4194304 | tf_op jit(solution)/shard_map/all_gather | solution.py:104
  511.1 9.8 %reshape.223 = bf16[32,2,16384]{2,1,0:T(2,128)(2,1)} reshape(bf16[8192,2,64]{2,1,0:T(2,128)(2,1)} %bitcast.54) | data formatting | bytes 4194304
  521.0 4.9 all-to-all-start.1
  525.9 0.0 all-gather.13.cloned.1.call-start
  525.9 0.7 convert_element_type.78
  526.7 0.0 all-gather.13.cloned.1.call-update
  526.7 0.3 reduce-scatter.5.cloned.1.call-start
  527.0 22.9 %all-to-all-done.1 = bf16[32,2,16384]{2,1,0:T(2,128)(2,1)S(1)} async-done(((bf16[32,2,16384]{2,1,0:T(2,128)(2,1)}), bf16[32,2,16384]{2,1,0:T(2,128)(2,1)S(1)}, u32[]{:S(2)}, u32[]{:S(2)}) %all-to-all-start.1) | async-done | bytes 2097184 | tf_op jit(solution)/shard_map/all_to_all | solution.py:110
  549.9 4.0 reshape.224
  554.0 6.4 copy.40
  560.4 0.2 fusion.65
  560.5 0.6 copy.38
  561.1 0.6 copy.39
  561.7 32.2 %all-gather.9.cloned.1.call-done = bf16[1280,2048]{1,0:T(8,128)(2,1)} async-done(((bf16[40,2048]{1,0:T(8,128)(2,1)}), bf16[1280,2048]{1,0:T(8,128)(2,1)}) %all-gather.9.cloned.1.call-update) | async-done | bytes 5242896 | tf_op jit(solution)/shard_map/all_gather | solution.py:165
  593.9 6.9 fusion.9
  600.7 12.4 %all-gather.13.cloned.1.call-done = bf16[256,2048]{1,0:T(8,128)(2,1)} async-done(((bf16[64,2048]{1,0:T(8,128)(2,1)}), bf16[256,2048]{1,0:T(8,128)(2,1)}) %all-gather.13.cloned.1.call-update) | async-done | bytes 1048592 | tf_op jit(solution)/shard_map/all_gather | solution.py:105
  613.2 5.9 convolution_convert_fusion
  619.1 0.0 reduce-scatter.5.cloned.1.call-update
  619.1 196.5 %reduce-scatter.5.cloned.1.call-done = bf16[40,2048]{1,0:T(8,128)(2,1)} async-done(((bf16[1280,2048]{1,0:T(8,128)(2,1)}), bf16[40,2048]{1,0:T(8,128)(2,1)}) %reduce-scatter.5.cloned.1.call-update) | async-done | bytes 163856 | tf_op jit(solution)/shard_map/reduce_scatter | solution.py:173
  815.6 1.1 fusion.34
  816.6 1.7 fusion.37
  (34 shorter events, 0.2 us)
Async XLA Ops:
  7.4 97.0 %all-gather.7.cloned.1.call-start = ((), (), s32[]{:S(2)}) async-start(), calls=%async_computation.4 | async-start | bytes 5406720 | tf_op jit(solution)/shard_map/all_gather | solution.py:126
  18.8 15.9 %copy-start.9 = (s32[1,8]{1,0:T(1,128)S(1)}, s32[1,8]{1,0:T(1,128)}, u32[]{:S(2)}) copy-start(s32[1,8]{1,0:T(1,128)} %param.14) | copy-start | bytes 100
  18.8 16.1 %copy-start.5 = (f32[16,2048]{1,0:T(8,128)S(1)}, f32[16,2048]{1,0:T(8,128)}, u32[]{:S(2)}) copy-start(f32[16,2048]{1,0:T(8,128)} %param.22) | copy-start | bytes 393220
  22.6 27.7 %all-to-all-start = ((bf16[32,2,6144]{2,1,0:T(2,128)(2,1)}), bf16[32,2,6144]{2,1,0:T(2,128)(2,1)S(1)}, u32[]{:S(2)}, u32[]{:S(2)}) async-start(bf16[32,2,6144]{2,1,0:T(2,128)(2,1)} %reshape.221), calls=%async_computation | async-start | bytes 1572864 | tf_op jit(solution)/shard_map/all_to_all | solution.py:109
  33.1 465.6 %reduce-scatter.3.cloned.1.call-start = ((), (), s32[]{:S(2)}) async-start(), calls=%async_computation.5 | async-start | bytes 5406720 | tf_op jit(solution)/shard_map/reduce_scatter | solution.py:155
  56.9 22.1 %collective-permute-start = (bf16[3,2048,64]{1,2,0:T(8,128)(2,1)S(1)}, bf16[3,2048,64]{1,2,0:T(8,128)(2,1)S(1)}, u32[]{:S(2)}, u32[]{:S(2)}) collective-permute-start(bf16[3,2048,64]{1,2,0:T(8,128)(2,1)S(1)} %all_to_all.27), channel_id=1, source_target_pairs={{0,1},{1,0},{2,3},{3,2},{4,5},{5,4},{6,7},{7,6},{8,9},{9,8},{10,11... | collective-permute-start | bytes 2359304 | tf_op jit(solution)/shard_map/ppermute | solution.py:22
  78.9 0.9 copy-start.8
  300.8 1.0 copy-start.2
  300.8 1.2 copy-start.3
  300.8 199.0 %copy-start.1 = (bf16[40,2048]{1,0:T(8,128)(2,1)S(1)}, bf16[40,2048]{1,0:T(8,128)(2,1)}, u32[]{:S(2)}) copy-start(bf16[40,2048]{1,0:T(8,128)(2,1)} %param.13) | copy-start | bytes 491524
  300.8 199.0 %copy-start.6 = (f32[2048]{0:T(1024)S(1)}, f32[2048]{0:T(1024)}, u32[]{:S(2)}) copy-start(f32[2048]{0:T(1024)} %param.17) | copy-start | bytes 24580
  300.8 200.8 %all-gather.11.cloned.1.call-start = ((), (), s32[]{:S(2)}) async-start(), calls=%async_computation.7 | async-start | bytes 2621440 | tf_op jit(solution)/shard_map/all_gather | solution.py:104
  302.9 291.0 %all-gather.9.cloned.1.call-start = ((), (), s32[]{:S(2)}) async-start(), calls=%async_computation.6 | async-start | bytes 5406720 | tf_op jit(solution)/shard_map/all_gather | solution.py:165
  521.0 5.0 copy-start.4
  521.0 29.0 %all-to-all-start.1 = ((bf16[32,2,16384]{2,1,0:T(2,128)(2,1)}), bf16[32,2,16384]{2,1,0:T(2,128)(2,1)S(1)}, u32[]{:S(2)}, u32[]{:S(2)}) async-start(bf16[32,2,16384]{2,1,0:T(2,128)(2,1)} %reshape.223), calls=%async_computation.2 | async-start | bytes 4194304 | tf_op jit(solution)/shard_map/all_to_all | solution.py:110
  525.9 87.3 %all-gather.13.cloned.1.call-start = ((), (), s32[]{:S(2)}) async-start(), calls=%async_computation.9 | async-start | bytes 1310720 | tf_op jit(solution)/shard_map/all_gather | solution.py:105
  526.7 288.8 %reduce-scatter.5.cloned.1.call-start = ((), (), s32[]{:S(2)}) async-start(), calls=%async_computation.8 | async-start | bytes 5406720 | tf_op jit(solution)/shard_map/reduce_scatter | solution.py:173
  619.1 197.6 %copy-start = (bf16[40,2048]{1,0:T(8,128)(2,1)S(1)}, bf16[40,2048]{1,0:T(8,128)(2,1)}, u32[]{:S(2)}) copy-start(bf16[40,2048]{1,0:T(8,128)(2,1)} %fusion.33) | copy-start | bytes 491524
  619.1 197.6 %copy-start.7 = (f32[2048]{0:T(1024)S(1)}, f32[2048]{0:T(1024)}, u32[]{:S(2)}) copy-start(f32[2048]{0:T(1024)} %param.18) | copy-start | bytes 24580
Sparse Core Ops, SparseCore 0:
  11.3 93.0 all-gather.6
  300.9 197.7 reduce-scatter.2
Sparse Core Ops, SparseCore 1:
  303.0 30.8 all-gather.10
  501.6 92.2 all-gather.8
  595.4 17.7 all-gather.12
  619.2 196.3 reduce-scatter.4
where the time goes:
time: 827 us; the launch traced here: 826 us
  waiting for transfers between devices  508 us (61%)
  blocking collectives  196 us (24%)
  local copies, waits for them, and re-layouts  52.2 us (6%)
  matrix products  24.7 us (3%)
  starting transfers between devices  16.9 us (2%)
  between operations  15.4 us (2%)
  other arithmetic  12.3 us (1%)
    reduce_scatter x1, waiting for transfers between devices, per_device(): lax.psum_scatter(jnp.dot(rows_part, down_block, preferred_element_type=jn...  196 us
    reduce_scatter x1, waiting for transfers between devices, per_device(): lax.psum_scatter(jnp.dot(rows_part, output_block, preferred_element_type=...  196 us
    psum x1, blocking collectives, per_device(): query_total, key_total = lax.psum((query_sq, key_sq), 'mp')  182 us
    all_gather x1, waiting for transfers between devices, per_device(): lax.all_gather(hidden, 'mp', axis=0, tiled=True)  32.2 us
    all_gather x1, waiting for transfers between devices, per_device(): lax.all_gather(tokens, 'mp', axis=0, tiled=True)  24.5 us
    all_to_all x1, waiting for transfers between devices, per_device(): lax.all_to_all(mlp_rows, 'mp', split_axis=2, concat_axis=1, tiled=True)  22.9 us
    ppermute x1, waiting for transfers between devices, partner_2(): return lax.ppermute(block, axis, route)  20.9 us
    unnamed x24, local copies, waits for them, and re-layouts  19.6 us
  transfers between devices with their start and end apart: 9, of which 8 were waited for; matrix products, arithmetic and copies ran while one was open for 7% of the time, Pallas kernels for 0%

commit v1 on v0

v1 whole, which is shorter than its diff:
```python
import math

import jax
import jax.numpy as jnp
from jax import lax
from jax.sharding import Mesh, PartitionSpec as P

HEAD_DIM = 128
NORM_EPSILON = 1e-06
ROPE_BASE = 500000.0
PLANE = ("z", "x")
COLUMN = ("yhi", "ylo", "core")


def segments(prompt_lens, rows):
    seg_ends = jnp.cumsum(prompt_lens)
    starts = seg_ends - prompt_lens
    segment = jnp.sum((rows[:, None] >= seg_ends[None, :]).astype(jnp.int32), axis=1)
    member = segment[:, None] == jnp.arange(prompt_lens.shape[0], dtype=jnp.int32)[None, :]
    opening = jnp.sum(jnp.where(member, starts[None, :], 0), axis=1)
    return segment, rows - opening


def rotary(values_in, cosines, sines):
    half = HEAD_DIM // 2
    front, back = values_in[:, :half], values_in[:, half:]
    return jnp.concatenate(
        [front * cosines - back * sines, back * cosines + front * sines], axis=-1
    )


def rms_scale(values_in, gain):
    return (
        values_in
        * lax.rsqrt(jnp.mean(values_in * values_in, axis=-1, keepdims=True) + NORM_EPSILON)
        * gain
    )


def sum_scatter(partial, tok_rows):
    blocks = partial.astype(jnp.bfloat16).reshape(-1, tok_rows, partial.shape[1])
    got = lax.all_to_all(blocks, PLANE, split_axis=0, concat_axis=0, tiled=True)
    return jnp.sum(got.astype(jnp.float32), axis=0)


def column_blocks(weights, parts):
    rows = weights[0].shape[0]
    split = [w.astype(jnp.bfloat16).reshape(rows, parts, -1) for w in weights]
    blocks = jnp.concatenate(split, axis=2).transpose(1, 0, 2)
    got = lax.all_to_all(blocks, PLANE, split_axis=0, concat_axis=0, tiled=True)
    whole = lax.all_gather(got, COLUMN, axis=1, tiled=True)
    return whole.reshape(-1, whole.shape[2])


def row_blocks(weight):
    return lax.all_gather(weight.astype(jnp.bfloat16), COLUMN, axis=0, tiled=True)


def per_device(
    tokens,
    lengths,
    query_gain,
    key_gain,
    attn_post_gain,
    mlp_post_gain,
    query_weight,
    key_weight,
    value_weight,
    output_weight,
    gate_weight,
    up_weight,
    down_weight,
):
    features = tokens.shape[1]
    parts = lax.axis_size("z") * lax.axis_size("x")
    place = lax.axis_index("z") * lax.axis_size("x") + lax.axis_index("x")
    half = lax.axis_index("yhi")
    tok_rows = tokens.shape[0]
    set_rows = tok_rows * parts
    qkv = column_blocks([query_weight, key_weight, value_weight], parts)
    output_block = row_blocks(output_weight)
    mlp_weights = column_blocks([gate_weight, up_weight], parts)
    down_block = row_blocks(down_weight)
    gathered = lax.all_gather(tokens, PLANE, axis=0, tiled=True)
    projected = jnp.dot(gathered, qkv, preferred_element_type=jnp.float32)
    q_raw, k_raw, v_raw = jnp.split(projected, 3, axis=1)
    squares = jnp.stack([jnp.sum(q_raw * q_raw, axis=1), jnp.sum(k_raw * k_raw, axis=1)])
    totals = jnp.sum(lax.all_gather(squares, PLANE, axis=0, tiled=False), axis=0)
    q_part = lax.dynamic_slice_in_dim(query_gain, place * HEAD_DIM, HEAD_DIM)
    k_part = lax.dynamic_slice_in_dim(key_gain, place * HEAD_DIM, HEAD_DIM)
    q_normed = q_raw * lax.rsqrt(totals[0] / features + NORM_EPSILON)[:, None] * q_part
    k_normed = k_raw * lax.rsqrt(totals[1] / features + NORM_EPSILON)[:, None] * k_part
    index = jnp.arange(set_rows, dtype=jnp.int32)

    def rows_of(which):
        return (index // tok_rows * 2 + which) * tok_rows + index % tok_rows

    my_rows = rows_of(half)
    segment, position = segments(lengths[0], my_rows)
    frequency = jnp.exp(
        jnp.arange(HEAD_DIM // 2, dtype=jnp.float32) * (-2.0 * math.log(ROPE_BASE) / HEAD_DIM)
    )
    angles = position.astype(jnp.float32)[:, None] * frequency[None, :]
    cosines, sines = jnp.cos(angles), jnp.sin(angles)
    queries = rotary(q_normed, cosines, sines).astype(jnp.bfloat16)
    keys_rot = rotary(k_normed, cosines, sines).astype(jnp.bfloat16)
    kv_mine = jnp.concatenate([keys_rot, v_raw.astype(jnp.bfloat16)], axis=1)
    kv_other = lax.ppermute(kv_mine, "yhi", [(0, 1), (1, 0)])
    kv = jnp.concatenate([kv_mine, kv_other], axis=0)
    key_rows = jnp.concatenate([my_rows, rows_of(1 - half)])
    key_segment, _ = segments(lengths[0], key_rows)
    scores = lax.dot_general(
        queries, kv[:, :HEAD_DIM], (((1,), (1,)), ((), ())), preferred_element_type=jnp.float32
    ) * (1.0 / math.sqrt(HEAD_DIM))
    allowed = (segment[:, None] == key_segment[None, :]) & (key_rows[None, :] <= my_rows[:, None])
    scores = jnp.where(allowed, scores, -1e30)
    weights = jnp.exp(scores - jnp.max(scores, axis=1, keepdims=True))
    weights = weights / jnp.sum(weights, axis=1, keepdims=True)
    attended = jnp.dot(
        weights.astype(jnp.bfloat16), kv[:, HEAD_DIM:], preferred_element_type=jnp.float32
    ).astype(jnp.bfloat16)
    attn_out = sum_scatter(
        jnp.dot(attended, output_block, preferred_element_type=jnp.float32), tok_rows
    )
    hidden = (tokens.astype(jnp.float32) + rms_scale(attn_out, attn_post_gain)).astype(jnp.bfloat16)
    both_proj = jnp.dot(
        lax.all_gather(hidden, PLANE, axis=0, tiled=True),
        mlp_weights,
        preferred_element_type=jnp.float32,
    )
    width = both_proj.shape[1] // 2
    activated = (jax.nn.silu(both_proj[:, :width]) * both_proj[:, width:]).astype(jnp.bfloat16)
    mlp_out = sum_scatter(
        jnp.dot(activated, down_block, preferred_element_type=jnp.float32), tok_rows
    )
    return (hidden.astype(jnp.float32) + rms_scale(mlp_out, mlp_post_gain)).astype(jnp.bfloat16)


def solution(mesh):
    fine = Mesh(mesh.devices.reshape(2, 2, 4, 4, 2), ("ylo", "core", "z", "x", "yhi"))
    tok = P(("ylo", "core", "z", "x", "yhi"), None)
    weight = P(("z", "x", "yhi", "ylo", "core"), None)
    return jax.shard_map(
        per_device,
        mesh=fine,
        in_specs=(tok, P(("ylo", "core"), None), P(), P(), P(), P()) + (weight,) * 7,
        out_specs=tok,
        check_vma=False,
    )
```

time: 827 us -> 316 us (0.38)
  waiting for transfers between devices: 508 us -> 117 us
  blocking collectives: 196 us -> 138 us
  local copies, waits for them, and re-layouts: 52.2 us -> 13.6 us
  starting transfers between devices: 16.9 us -> 7.01 us
    reduce_scatter x2 -> x0, waiting for transfers between devices: 392 us -> none  [the longest x1 196 us: per_device(): lax.psum_scatter(jnp.dot(rows_part, down_block, preferred_element_type=jn...]
    psum x1 -> x0, blocking collectives: 182 us -> none  [per_device(): query_total, key_total = lax.psum((query_sq, key_sq), 'mp')]
    all_to_all x0 -> x3, blocking collectives: none -> 98.1 us  [the longest x2 82 us: sum_scatter(): got = lax.all_to_all(blocks, PLANE, split_axis=0, concat_axis=0, tiled=True)]
    all_gather x4 -> x5, waiting for transfers between devices: 69.1 us -> 106 us  [the longest x1 46.8 us: per_device(): gathered = lax.all_gather(tokens, PLANE, axis=0, tiled=True)]
    all_gather x2, blocking collectives: 14.6 us -> 40.3 us  [the longest x1 22.9 us: per_device(): lax.all_gather(squares, PLANE, axis=0, tiled=False)]
    ppermute x1, waiting for transfers between devices: 20.9 us -> 0.01 us  [per_device(): kv_other = lax.ppermute(kv_mine, 'yhi', [(0, 1), (1, 0)])]
    unnamed x24 -> x25, local copies, waits for them, and re-layouts: 19.6 us -> 0.77 us
    all_to_all x2 -> x1, waiting for transfers between devices: 25.3 us -> 10.3 us  [column_blocks(): got = lax.all_to_all(blocks, PLANE, split_axis=0, concat_axis=0, tiled=True)]
  transfers between devices with their start and end apart: 9 -> 7, of which waited for: 8 -> 5; matrix products, arithmetic and copies ran while one was open for 7% -> 10% of each run, Pallas kernels for 0% -> 0%
where the time goes in v1:
time: 316 us; the launch traced here: 315 us
  blocking collectives  138 us (44%)
  waiting for transfers between devices  117 us (37%)
  matrix products  17.6 us (6%)
  local copies, waits for them, and re-layouts  13.6 us (4%)
  between operations  13.5 us (4%)
  other arithmetic  8.72 us (3%)
  starting transfers between devices  7.01 us (2%)
    all_to_all x2, blocking collectives, sum_scatter(): got = lax.all_to_all(blocks, PLANE, split_axis=0, concat_axis=0, tiled=True)  82 us
    all_gather x1, waiting for transfers between devices, per_device(): gathered = lax.all_gather(tokens, PLANE, axis=0, tiled=True)  46.8 us
    all_gather x1, waiting for transfers between devices, per_device(): lax.all_gather(hidden, PLANE, axis=0, tiled=True)  35.2 us
    all_gather x1, blocking collectives, per_device(): lax.all_gather(squares, PLANE, axis=0, tiled=False)  22.9 us
    all_gather x1, waiting for transfers between devices, row_blocks(): lax.all_gather(weight.astype(jnp.bfloat16), COLUMN, axis=0, tiled=True)  20.6 us
    all_gather x1, blocking collectives, row_blocks(): lax.all_gather(weight.astype(jnp.bfloat16), COLUMN, axis=0, tiled=True)  17.3 us
    all_to_all x1, blocking collectives, column_blocks(): got = lax.all_to_all(blocks, PLANE, split_axis=0, concat_axis=0, tiled=True)  16.1 us
    all_to_all x1, waiting for transfers between devices, column_blocks(): got = lax.all_to_all(blocks, PLANE, split_axis=0, concat_axis=0, tiled=True)  10.3 us
  transfers between devices with their start and end apart: 7, of which 5 were waited for; matrix products, arithmetic and copies ran while one was open for 10% of the time, Pallas kernels for 0%

profile of v1, /device:TPU:0, one launch (start us, length us, event | category | flops | bytes accessed | tf_op | source)
XLA Modules:
  0.0 315.3 jit_solution(8745225860466606189)
XLA Ops:
  6.5 0.0 all-gather.8.cloned.1.call-start
  6.5 1.0 convert_bitcast_fusion.2
  7.6 0.9 convert_bitcast_fusion.1
  8.5 0.9 convert_bitcast_fusion
  9.5 16.1 %all_to_all.20 = bf16[16,16,384]{2,1,0:T(8,128)(2,1)S(1)} all-to-all(bf16[16,16,384]{2,1,0:T(8,128)(2,1)S(1)} %copy.22), channel_id=1, replica_groups=mesh['ylo'=2,'core'=2,'z'=4,'x'=4,'yhi'=2] {'z','x'}, dimensions={0} | all-to-all | bytes 393216 | tf_op jit(solution)/shard_map/all_to_all | solution.py:50
  25.6 0.7 copy.23
  26.4 0.0 all-gather.8.cloned.1.call-update
  26.4 0.0 all-gather.10.cloned.1.call-start
  26.4 0.7 all-gather.10.cloned.1.call-update
  27.2 0.1 copy.31
  27.3 0.0 copy-done.4
  27.3 0.0 copy-start.9
  27.3 0.0 copy-start.6
  27.3 0.1 copy.32
  27.4 0.1 maximum_bitcast_fusion
  27.5 1.1 copy.25
  28.6 3.6 %all-to-all-start.2 = ((bf16[16,16,1024]{2,1,0:T(8,128)(2,1)}), bf16[16,16,1024]{2,1,0:T(8,128)(2,1)S(1)}, u32[]{:S(2)}, u32[]{:S(2)}) async-start(bf16[16,16,1024]{2,1,0:T(8,128)(2,1)} %copy.25), calls=%async_computation.2 | async-start | bytes 1048576 | tf_op jit(solution)/shard_map/all_to_all | solution.py:50
  32.2 0.0 all-gather.14.cloned.1.call-start
  32.3 10.3 %all-to-all-done.2 = bf16[16,16,1024]{2,1,0:T(8,128)(2,1)S(1)} async-done(((bf16[16,16,1024]{2,1,0:T(8,128)(2,1)}), bf16[16,16,1024]{2,1,0:T(8,128)(2,1)S(1)}, u32[]{:S(2)}, u32[]{:S(2)}) %all-to-all-start.2) | async-done | bytes 524320 | tf_op jit(solution)/shard_map/all_to_all | solution.py:50
  42.6 1.1 copy.26
  43.7 0.0 all-gather.14.cloned.1.call-update
  43.7 0.0 all-gather.12.cloned.1.call-start
  43.8 0.8 dynamic_slice.6
  44.6 0.8 dynamic_slice.7
  45.3 0.2 reduce-window.4
  45.5 0.0 copy-done.6
  45.5 0.1 convert_reduce_fusion.3
  45.6 0.1 select_reduce_fusion
  45.7 3.0 all-gather.8.cloned.1.call-done
  48.7 1.8 copy.24
  50.5 46.8 %all-gather.10.cloned.1.call-done = bf16[640,2048]{1,0:T(8,128)(2,1)} async-done(((bf16[40,2048]{1,0:T(8,128)(2,1)}), bf16[640,2048]{1,0:T(8,128)(2,1)}) %all-gather.10.cloned.1.call-update) | async-done | bytes 2621456 | tf_op jit(solution)/shard_map/all_gather | solution.py:84
  97.3 3.2 %convolution_bitcast_fusion = f32[640,384]{0,1:T(8,128)S(1)} fusion(bf16[2048,384]{1,0:T(8,128)(2,1)S(1)} %bitcast.42, bf16[640,2048]{1,0:T(8,128)(2,1)} %all-gather.10.cloned.1.call-done), kind=kOutput, calls=%fused_computation.10 | convolution fusion | flops 1006632960 | bytes 5177344 | tf_op jit(solution)/shard_map/dot_general | solution.py:85
  100.5 0.1 multiply_reduce_fusion.3
  100.6 22.9 %all-gather.1 = f32[16,2,640]{2,1,0:T(2,128)S(1)} all-gather(f32[1,2,640]{2,1,0:T(2,128)S(1)} %maximum_bitcast_fusion.2), channel_id=2, replica_groups=mesh['ylo'=2,'core'=2,'z'=4,'x'=4,'yhi'=2] {'z','x'}, dimensions={0}, use_global_device_ids=true | all-gather | bytes 87040 | tf_op jit(solution)/shard_map/all_gather | solution.py:88
  123.6 0.1 multiply_multiply_fusion.1
  123.7 0.7 fusion.19
  124.5 3.1 collective-permute-start
  127.6 0.1 convert_reduce_fusion.2
  127.7 17.3 %all_gather.28 = bf16[128,2048]{1,0:T(8,128)(2,1)} all-gather(bf16[16,2048]{1,0:T(8,128)(2,1)S(1)} %convert_element_type.79), channel_id=1, replica_groups=mesh['ylo'=2,'core'=2,'z'=4,'x'=4,'yhi'=2] {'yhi','ylo','core'}, dimensions={0}, use_global_device_ids=true | all-gather | bytes 589824 | tf_op jit(solution)/shard_map/all_gather | solution.py:56
  145.0 0.0 collective-permute-done
  145.1 1.0 fusion.48
  146.1 0.6 fusion.1
  146.7 4.9 %convolution_convert_fusion.1 = bf16[640,2048]{1,0:T(8,128)(2,1)} fusion(bf16[128,2048]{1,0:T(8,128)(2,1)} %all_gather.28, f32[640,1280]{1,0:T(8,128)S(1)} %get-tuple-element.18, f32[640]{0:T(1024)S(1)} %fusion.1, f32[640]{0:T(1024)S(1)} %get-tuple-element.17, bf16[1280,256]{0,1:T(8,128)(2,1)} %copy-done.1), kind=kOutput, calls=%fused_computation.7 | convolution fusion | flops 549109760 | bytes 6755328 | tf_op jit(solution)/shard_map/dot_general | solution.py:123
  151.6 40.8 %all_to_all.21 = bf16[16,40,2048]{2,1,0:T(8,128)(2,1)S(1)} all-to-all(bf16[16,40,2048]{2,1,0:T(8,128)(2,1)} %bitcast.40), channel_id=1, replica_groups=mesh['ylo'=2,'core'=2,'z'=4,'x'=4,'yhi'=2] {'z','x'}, dimensions={0} | all-to-all | bytes 5242880 | tf_op jit(solution)/shard_map/all_to_all | solution.py:42
  192.4 0.5 convert_reduce_fusion.1
  192.9 0.1 multiply_reduce_fusion.1
  193.0 0.3 copy-done.2
  193.3 0.8 add_convert_fusion.1
  194.1 0.0 all-gather.12.cloned.1.call-update
  194.1 0.2 all-gather.16.cloned.1.call-start
  194.4 0.7 convert_element_type.87
  195.1 0.0 all-gather.16.cloned.1.call-update
  195.1 0.0 all-gather.14.cloned.1.call-done
  195.1 6.5 %copy.27 = bf16[16,128,1024]{2,1,0:T(8,128)(2,1)} copy(bf16[16,128,1024]{2,0,1:T(8,128)(2,1)} %all-gather.14.cloned.1.call-done) | data formatting | bytes 8388608 | tf_op jit(solution)/shard_map/all_gather | solution.py:51
  201.6 35.2 %all-gather.12.cloned.1.call-done = bf16[640,2048]{1,0:T(8,128)(2,1)} async-done(((bf16[40,2048]{1,0:T(8,128)(2,1)}), bf16[640,2048]{1,0:T(8,128)(2,1)}) %all-gather.12.cloned.1.call-update) | async-done | bytes 2621456 | tf_op jit(solution)/shard_map/all_gather | solution.py:127
  236.8 5.4 %fusion.49 = f32[640,1024]{1,0:T(8,128)S(1)} fusion(bf16[640,2048]{1,0:T(8,128)(2,1)} %all-gather.12.cloned.1.call-done, bf16[2048,1024]{1,0:T(8,128)(2,1)} %bitcast.39), kind=kOutput, calls=%fused_computation.91 | convolution fusion | flops 2684354560 | bytes 9437184 | tf_op jit(solution)/shard_map/dot_general | solution.py:126
  242.2 20.6 %all-gather.16.cloned.1.call-done = bf16[512,2048]{1,0:T(8,128)(2,1)} async-done(((bf16[64,2048]{1,0:T(8,128)(2,1)}), bf16[512,2048]{1,0:T(8,128)(2,1)}) %all-gather.16.cloned.1.call-update) | async-done | bytes 2097168 | tf_op jit(solution)/shard_map/all_gather | solution.py:56
  262.8 3.1 convolution_convert_fusion
  265.9 41.2 %all_to_all.22 = bf16[16,40,2048]{2,1,0:T(8,128)(2,1)S(1)} all-to-all(bf16[16,40,2048]{2,1,0:T(8,128)(2,1)S(1)} %bitcast.41), channel_id=1, replica_groups=mesh['ylo'=2,'core'=2,'z'=4,'x'=4,'yhi'=2] {'z','x'}, dimensions={0} | all-to-all | bytes 5242880 | tf_op jit(solution)/shard_map/all_to_all | solution.py:42
  307.1 0.5 convert_reduce_fusion
  307.6 0.1 multiply_reduce_fusion
  307.8 0.3 copy-done
  308.0 0.0 copy-done.8
  308.0 0.8 add_convert_fusion
  (37 shorter events, 0.5 us)
Async XLA Ops:
  6.5 20.6 %copy-start.3 = (f32[16,8192]{1,0:T(8,128)S(1)}, f32[16,8192]{1,0:T(8,128)}, u32[]{:S(2)}) copy-start(f32[16,8192]{1,0:T(8,128)} %param.23) | copy-start | bytes 1572868
  6.5 20.7 %copy-start.4 = (f32[16,8192]{1,0:T(8,128)S(1)}, f32[16,8192]{1,0:T(8,128)}, u32[]{:S(2)}) copy-start(f32[16,8192]{1,0:T(8,128)} %param.24) | copy-start | bytes 1572868
  6.5 42.2 %all-gather.8.cloned.1.call-start = ((), (), s32[]{:S(2)}) async-start(), calls=%async_computation.4 | async-start | bytes 1769472 | tf_op jit(solution)/shard_map/all_gather | solution.py:51
  26.4 70.9 %all-gather.10.cloned.1.call-start = ((), (), s32[]{:S(2)}) async-start(), calls=%async_computation.5 | async-start | bytes 2785280 | tf_op jit(solution)/shard_map/all_gather | solution.py:84
  27.3 18.0 %copy-start.9 = (s32[1,8]{1,0:T(1,128)S(1)}, s32[1,8]{1,0:T(1,128)}, u32[]{:S(2)}) copy-start(s32[1,8]{1,0:T(1,128)} %param.14) | copy-start | bytes 100
  27.3 18.2 %copy-start.6 = (f32[16,2048]{1,0:T(8,128)S(1)}, f32[16,2048]{1,0:T(8,128)}, u32[]{:S(2)}) copy-start(f32[16,2048]{1,0:T(8,128)} %param.22) | copy-start | bytes 393220
  28.6 14.0 %all-to-all-start.2 = ((bf16[16,16,1024]{2,1,0:T(8,128)(2,1)}), bf16[16,16,1024]{2,1,0:T(8,128)(2,1)S(1)}, u32[]{:S(2)}, u32[]{:S(2)}) async-start(bf16[16,16,1024]{2,1,0:T(8,128)(2,1)} %copy.25), calls=%async_computation.2 | async-start | bytes 1048576 | tf_op jit(solution)/shard_map/all_to_all | solution.py:50
  32.2 163.0 %all-gather.14.cloned.1.call-start = ((), (), s32[]{:S(2)}) async-start(), calls=%async_computation.7 | async-start | bytes 4718592 | tf_op jit(solution)/shard_map/all_gather | solution.py:51
  43.7 193.1 %all-gather.12.cloned.1.call-start = ((), (), s32[]{:S(2)}) async-start(), calls=%async_computation.6 | async-start | bytes 2785280 | tf_op jit(solution)/shard_map/all_gather | solution.py:127
  124.5 20.5 %collective-permute-start = (bf16[640,256]{0,1:T(8,128)(2,1)S(1)}, bf16[640,256]{0,1:T(8,128)(2,1)S(1)}, u32[]{:S(2)}, u32[]{:S(2)}) collective-permute-start(bf16[640,256]{0,1:T(8,128)(2,1)S(1)} %pad_maximum_fusion.1), channel_id=1, source_target_pairs={{0,1},{1,0},{2,3},{3,2},{4,5},{5,4},{6,7},{7,6},{8,9},{9,8},{10,11... | collective-permute-start | bytes 983048 | tf_op jit(solution)/shard_map/ppermute | solution.py:108
  145.1 1.1 copy-start.1
  192.4 0.9 copy-start.2
  192.4 0.9 copy-start.7
  192.4 2.0 copy-start.5
  194.1 68.7 %all-gather.16.cloned.1.call-start = ((), (), s32[]{:S(2)}) async-start(), calls=%async_computation.8 | async-start | bytes 2359296 | tf_op jit(solution)/shard_map/all_gather | solution.py:56
  307.1 0.9 copy-start
  307.1 0.9 copy-start.8
Sparse Core Ops, SparseCore 0:
  26.5 22.1 all-gather.7
  50.9 46.3 all-gather.9
  99.0 36.7 all-gather.13
  194.2 42.4 all-gather.11
  238.3 24.4 all-gather.15

commit v2 on v1

v2 whole, which is shorter than its diff:
```python
import math

import jax
import jax.numpy as jnp
from jax import lax
from jax.experimental import pallas as pl
from jax.experimental.pallas import tpu as pltpu
from jax.sharding import Mesh, PartitionSpec as P

HEAD_DIM = 128
NORM_EPSILON = 1e-06
ROPE_BASE = 500000.0
SIDE = 4
PLANE = SIDE * SIDE
COLUMN = 8
MESH = pl.DeviceIdType.MESH
F32 = jnp.float32
BF16 = jnp.bfloat16
HIGHEST = lax.Precision.HIGHEST


def remote(src, dst, send_sem, recv_sem, device):
    return pltpu.make_async_remote_copy(
        src_ref=src,
        dst_ref=dst,
        send_sem=send_sem,
        recv_sem=recv_sem,
        device_id=device,
        device_id_type=MESH,
    )


def plane_device(place):
    return {"z": place // SIDE, "x": lax.rem(place, SIDE)}


def dot(a, b):
    return jnp.dot(a, b, preferred_element_type=F32)


def kernel(
    lengths,
    tokens,
    query_gain,
    key_gain,
    attn_gain,
    mlp_gain,
    query_w,
    key_w,
    value_w,
    output_w,
    gate_w,
    up_w,
    down_w,
    out,
    stage_qkv,
    stage_mlp,
    qkv_all,
    mlp_all,
    out_all,
    down_all,
    tok_all,
    x_rows,
    proj,
    sq_all,
    kv,
    queries,
    cosines,
    sines,
    opening,
    part_a,
    got_a,
    hid_all,
    part_b,
    got_b,
    act,
    total,
    s_qkv,
    r_qkv,
    s_tok,
    r_tok,
    s_mlp,
    r_mlp,
    s_sq,
    r_sq,
    s_pa,
    r_pa,
    s_hid,
    r_hid,
    s_pb,
    r_pb,
    c_send,
    c_recv,
    s_kv,
    r_kv,
):
    z, x = lax.axis_index("z"), lax.axis_index("x")
    yhi, ylo, core = lax.axis_index("yhi"), lax.axis_index("ylo"), lax.axis_index("core")
    me = z * SIDE + x
    y = yhi * 2 + ylo
    slot = y * 2 + core
    rows = tokens.shape[0]
    set_rows = rows * PLANE
    group_rows = rows * SIDE
    features = tokens.shape[1]
    hidden_width = act.shape[1]

    def y_peer(step):
        other = lax.rem(y + step, SIDE)
        return other, {"yhi": other // 2, "ylo": lax.rem(other, 2)}

    sibling = {"core": 1 - core}

    barrier = pltpu.get_barrier_semaphore()

    @pl.loop(1, PLANE)
    def _(i):
        pl.semaphore_signal(
            barrier, inc=1, device_id=plane_device(lax.rem(me + i, PLANE)), device_id_type=MESH
        )

    @pl.loop(1, SIDE)
    def _(i):
        pl.semaphore_signal(barrier, inc=1, device_id=y_peer(i)[1], device_id_type=MESH)

    pl.semaphore_signal(barrier, inc=1, device_id=sibling, device_id_type=MESH)

    for p in range(PLANE):
        cols = slice(p * HEAD_DIM, (p + 1) * HEAD_DIM)
        for k, w in enumerate((query_w, key_w, value_w)):
            stage_qkv[p, :, k * HEAD_DIM : (k + 1) * HEAD_DIM] = w[:, cols].astype(BF16)
    pl.semaphore_wait(barrier, PLANE - 1 + SIDE)

    def plane_copy(i, src, dst, send, recv):
        peer = lax.rem(me + i, PLANE)
        return remote(src(peer), dst(me), send.at[i], recv.at[me], plane_device(peer))

    def plane_start(src, dst, send, recv):
        @pl.loop(1, PLANE)
        def _(i):
            plane_copy(i, src, dst, send, recv).start()

    def plane_wait_send(src, dst, send, recv):
        @pl.loop(1, PLANE)
        def _(i):
            plane_copy(i, src, dst, send, recv).wait_send()

    def wait_from(peer, dst, send, recv):
        remote(dst(peer), dst(peer), send.at[0], recv.at[peer], plane_device(peer)).wait_recv()

    def plane_wait_recv(dst, send, recv):
        @pl.loop(1, PLANE)
        def _(i):
            wait_from(lax.rem(me + PLANE - i, PLANE), dst, send, recv)

    qkv_move = (lambda p: stage_qkv.at[p], lambda p: qkv_all.at[p, slot], s_qkv, r_qkv)
    plane_start(*qkv_move)
    tok_move = (lambda p: tokens, lambda p: tok_all.at[p], s_tok, r_tok)
    plane_start(*tok_move)
    qkv_all[me, slot] = stage_qkv[me]
    tok_all[me] = tokens[...]

    for p in range(PLANE):
        cols = slice(p * hidden_width, (p + 1) * hidden_width)
        for k, w in enumerate((gate_w, up_w)):
            stage_mlp[p, :, k * hidden_width : (k + 1) * hidden_width] = w[:, cols].astype(BF16)
    mlp_move = (lambda p: stage_mlp.at[p], lambda p: mlp_all.at[p, slot], s_mlp, r_mlp)
    plane_start(*mlp_move)
    mlp_all[me, slot] = stage_mlp[me]
    out_all[slot] = output_w[...].astype(BF16)
    down_all[slot] = down_w[...].astype(BF16)

    def column_y(kind, view, i):
        other, device = y_peer(i)
        return remote(view(slot), view(slot), c_send.at[kind, i], c_recv.at[kind, slot], device)

    def column_core(kind, view, i):
        held = y_peer(i)[0] * 2 + core
        return remote(
            view(held), view(held), c_send.at[kind, SIDE + i], c_recv.at[kind, held], sibling
        )

    def column_start(kind, view):
        @pl.loop(1, SIDE)
        def _(i):
            column_y(kind, view, i).start()

        column_core(kind, view, 0).start()

    def column_wait(kind, view, held):
        remote(
            view(held), view(held), c_send.at[kind, 0], c_recv.at[kind, held], sibling
        ).wait_recv()

    def column_pass(kind, view):
        @pl.loop(1, SIDE)
        def _(i):
            column_wait(kind, view, y_peer(i)[0] * 2 + core)
            column_core(kind, view, i).start()

    def column_finish(kind, view):
        @pl.loop(0, SIDE)
        def _(i):
            column_wait(kind, view, y_peer(i)[0] * 2 + 1 - core)

    def column_wait_send(kind, view):
        @pl.loop(1, SIDE)
        def _(i):
            column_y(kind, view, i).wait_send()

        @pl.loop(0, SIDE)
        def _(i):
            column_core(kind, view, i).wait_send()

    column = (
        (0, lambda q: qkv_all.at[:, q]),
        (1, lambda q: out_all.at[q]),
        (2, lambda q: mlp_all.at[:, q]),
        (3, lambda q: down_all.at[q]),
    )
    plane_wait_recv(*qkv_move[1:])
    column_start(*column[0])
    column_start(*column[1])

    def numbered(index, which):
        return index + ((index * 1639) >> 16) * rows + which * rows

    flat = lax.broadcasted_iota(jnp.int32, (set_rows, HEAD_DIM), 0)
    row = numbered(flat, yhi)
    start = jnp.zeros_like(row)
    end = jnp.int32(0)
    for r in range(lengths.shape[1]):
        end = end + lengths[0, r]
        start = start + jnp.where(row >= end, lengths[0, r], 0)
    opening[...] = start
    lane = lax.broadcasted_iota(jnp.int32, (1, HEAD_DIM), 1)
    half = HEAD_DIM // 2
    step = jnp.where(lane < half, lane, lane - half).astype(F32)
    frequency = jnp.exp(step * (-2.0 * math.log(ROPE_BASE) / HEAD_DIM))
    angle = (row - start).astype(F32) * frequency
    cosines[...] = jnp.cos(angle)
    sines[...] = jnp.sin(angle) * jnp.where(lane < half, -1.0, 1.0)

    column_pass(*column[0])
    plane_wait_recv(*mlp_move[1:])
    column_start(*column[2])
    column_start(*column[3])

    plane_wait_recv(*tok_move[1:])

    def pair(ref, first):
        return jnp.concatenate([ref[first].astype(F32), ref[first + 1].astype(F32)], axis=0).astype(
            BF16
        )

    @pl.loop(0, PLANE // 2)
    def _(j):
        x_rows[pl.ds(pl.multiple_of(j * 2 * rows, 2 * rows), 2 * rows), :] = pair(tok_all, 2 * j)

    column_finish(*column[0])

    def chunk(i):
        return pl.ds(pl.multiple_of(i * group_rows, group_rows), group_rows)

    @pl.loop(0, SIDE)
    def _(i):
        proj[chunk(i), :] = dot(x_rows[chunk(i), :], qkv_all[...].reshape(features, 3 * HEAD_DIM))

    both = proj[:, : 2 * HEAD_DIM]
    pick = (
        lax.broadcasted_iota(jnp.int32, (8, 2 * HEAD_DIM), 1) // HEAD_DIM
        == lax.broadcasted_iota(jnp.int32, (8, 2 * HEAD_DIM), 0)
    ).astype(F32)
    sq_all[me] = lax.dot_general(
        pick, both * both, (((1,), (1,)), ((), ())), precision=HIGHEST, preferred_element_type=F32
    )
    sq_move = (lambda p: sq_all.at[me], lambda p: sq_all.at[p], s_sq, r_sq)
    plane_start(*sq_move)
    kv[0, :, HEAD_DIM:] = proj[:, 2 * HEAD_DIM :].astype(BF16)
    plane_wait_recv(*sq_move[1:])
    sums = sq_all[0]
    for p in range(1, PLANE):
        sums = sums + sq_all[p]
    scale = jnp.transpose(lax.rsqrt(sums / features + NORM_EPSILON))

    def rotated(values_in, column_scale, gain):
        normed = values_in * column_scale * gain
        return normed * cosines[...] + pltpu.roll(normed, half, 1) * sines[...]

    kv[0, :, :HEAD_DIM] = rotated(
        proj[:, HEAD_DIM : 2 * HEAD_DIM], scale[:, 1:2], key_gain[...]
    ).astype(BF16)
    kv_copy = remote(kv.at[0], kv.at[1], s_kv, r_kv, {"yhi": 1 - yhi})
    kv_copy.start()
    queries[...] = rotated(proj[:, :HEAD_DIM], scale[:, 0:1], query_gain[...]).astype(BF16)
    column_pass(*column[1])
    column_finish(*column[1])
    kv_copy.wait_recv()

    lane_index = lax.broadcasted_iota(jnp.int32, (1, set_rows), 1)
    pa_move = (lambda p: part_a.at[p], lambda p: got_a.at[p], s_pa, r_pa)
    pb_move = (lambda p: part_b.at[p], lambda p: got_b.at[p], s_pb, r_pb)

    def send_group(group, part, got, send, recv):
        @pl.loop(0, SIDE)
        def _(b):
            peer = group * SIDE + lax.rem(x + b, SIDE)

            @pl.when(peer != me)
            def _():
                remote(
                    part.at[peer],
                    got.at[me],
                    send.at[lax.rem(peer - me + PLANE, PLANE)],
                    recv.at[me],
                    plane_device(peer),
                ).start()

    @pl.loop(1, SIDE + 1)
    def _(i):
        group = lax.rem(z + i, SIDE)
        here = chunk(group)
        key_row = jnp.concatenate([numbered(lane_index, yhi), numbered(lane_index, 1 - yhi)], axis=1)
        own = lax.broadcasted_iota(jnp.int32, (group_rows, 1), 0) + group * group_rows
        own_row = numbered(own, yhi)
        first = opening[here, :][:, 0:1]
        scores = lax.dot_general(
            queries[here, :],
            kv[:, :, :HEAD_DIM].reshape(2 * set_rows, HEAD_DIM),
            (((1,), (1,)), ((), ())),
            preferred_element_type=F32,
        ) * (1.0 / math.sqrt(HEAD_DIM))
        scores = jnp.where((key_row >= first) & (key_row <= own_row), scores, -1e30)
        weights = jnp.exp(scores - jnp.max(scores, axis=1, keepdims=True))
        weights = weights / jnp.sum(weights, axis=1, keepdims=True)
        attended = dot(
            weights.astype(BF16), kv[:, :, HEAD_DIM:].reshape(2 * set_rows, HEAD_DIM)
        ).astype(BF16)
        summed = dot(attended, out_all[...].reshape(HEAD_DIM, features))
        for b in range(SIDE):
            part_a[group * SIDE + b] = summed[b * rows : (b + 1) * rows].astype(BF16)
        send_group(group, part_a, got_a, s_pa, r_pa)

    got_a[me] = part_a[me]
    column_pass(*column[2])
    column_pass(*column[3])
    plane_wait_recv(*pa_move[1:])

    def summed_norm(got, gain):
        width = features // 4
        for c in range(4):
            cols = slice(c * width, (c + 1) * width)
            acc = got[0, :, cols].astype(F32)
            for p in range(1, PLANE):
                acc = acc + got[p, :, cols].astype(F32)
            total[:, cols] = acc
        values_in = total[...]
        mean = jnp.mean(values_in * values_in, axis=-1, keepdims=True)
        return values_in * lax.rsqrt(mean + NORM_EPSILON) * gain[...]

    hid_all[me] = (tokens[...].astype(F32) + summed_norm(got_a, attn_gain)).astype(BF16)
    hid_move = (lambda p: hid_all.at[me], lambda p: hid_all.at[p], s_hid, r_hid)
    plane_start(*hid_move)
    column_finish(*column[2])
    column_finish(*column[3])

    @pl.loop(0, SIDE)
    def _(i):
        group = lax.rem(z + i, SIDE)

        @pl.loop(0, SIDE)
        def _(b):
            peer = group * SIDE + b

            @pl.when(peer != me)
            def _():
                wait_from(peer, *hid_move[1:])

        values_in = jnp.concatenate(
            [pair(hid_all, group * SIDE), pair(hid_all, group * SIDE + 2)], axis=0
        )
        tile = 256
        for c in range(hidden_width // tile):
            lo = c * tile
            gate = dot(values_in, mlp_all[:, :, :, lo : lo + tile].reshape(features, tile))
            lo = lo + hidden_width
            up = dot(values_in, mlp_all[:, :, :, lo : lo + tile].reshape(features, tile))
            act[:, c * tile : (c + 1) * tile] = (gate / (1.0 + jnp.exp(-gate)) * up).astype(BF16)
        wide = 512
        for c in range(features // wide):
            cols = slice(c * wide, (c + 1) * wide)
            summed = dot(act[...], down_all[:, :, cols].reshape(hidden_width, wide))
            for b in range(SIDE):
                part_b[group * SIDE + b, :, cols] = summed[b * rows : (b + 1) * rows].astype(BF16)
        send_group(group, part_b, got_b, s_pb, r_pb)

    got_b[me] = part_b[me]
    plane_wait_recv(*pb_move[1:])
    out[...] = (hid_all[me].astype(F32) + summed_norm(got_b, mlp_gain)).astype(BF16)

    for move in (qkv_move, tok_move, mlp_move, sq_move, pa_move, hid_move, pb_move):
        plane_wait_send(*move)
    for kind, view in column:
        column_wait_send(kind, view)
    kv_copy.wait_send()


def per_device(tokens, lengths, query_gain, key_gain, attn_gain, mlp_gain, *weights):
    place = lax.axis_index("z") * SIDE + lax.axis_index("x")
    q_part = lax.dynamic_slice_in_dim(query_gain, place * HEAD_DIM, HEAD_DIM)[None]
    k_part = lax.dynamic_slice_in_dim(key_gain, place * HEAD_DIM, HEAD_DIM)[None]
    rows, features = tokens.shape
    depth = weights[0].shape[0]
    ff = weights[4].shape[1] // PLANE
    down_depth = weights[6].shape[0]
    set_rows = rows * PLANE
    vmem = pl.BlockSpec(memory_space=pltpu.VMEM)
    dma = pltpu.SemaphoreType.DMA
    blocks = (PLANE, rows, features)
    return pl.pallas_call(
        kernel,
        out_shape=jax.ShapeDtypeStruct(tokens.shape, BF16),
        in_specs=[pl.BlockSpec(memory_space=pltpu.SMEM)] + [vmem] * 12,
        out_specs=vmem,
        scratch_shapes=[
            pltpu.VMEM((PLANE, depth, 3 * HEAD_DIM), BF16),
            pltpu.VMEM((PLANE, depth, 2 * ff), BF16),
            pltpu.VMEM((PLANE, COLUMN, depth, 3 * HEAD_DIM), BF16),
            pltpu.VMEM((PLANE, COLUMN, depth, 2 * ff), BF16),
            pltpu.VMEM((COLUMN, depth, features), BF16),
            pltpu.VMEM((COLUMN, down_depth, features), BF16),
            pltpu.VMEM(blocks, BF16),
            pltpu.VMEM((set_rows, features), BF16),
            pltpu.VMEM((set_rows, 3 * HEAD_DIM), F32),
            pltpu.VMEM((PLANE, 8, set_rows), F32),
            pltpu.VMEM((2, set_rows, 2 * HEAD_DIM), BF16),
            pltpu.VMEM((set_rows, HEAD_DIM), BF16),
            pltpu.VMEM((set_rows, HEAD_DIM), F32),
            pltpu.VMEM((set_rows, HEAD_DIM), F32),
            pltpu.VMEM((set_rows, HEAD_DIM), jnp.int32),
            pltpu.VMEM(blocks, BF16),
            pltpu.VMEM(blocks, BF16),
            pltpu.VMEM(blocks, BF16),
            pltpu.VMEM(blocks, BF16),
            pltpu.VMEM(blocks, BF16),
            pltpu.VMEM((rows * SIDE, ff), BF16),
            pltpu.VMEM((rows, features), F32),
        ]
        + [dma((PLANE,))] * 14
        + [dma((4, COLUMN)), dma((4, COLUMN)), dma(()), dma(())],
        compiler_params=pltpu.CompilerParams(
            collective_id=0, has_side_effects=True, vmem_limit_bytes=60 << 20
        ),
    )(lengths, tokens, q_part, k_part, attn_gain[None], mlp_gain[None], *weights)


def solution(mesh):
    fine = Mesh(mesh.devices.reshape(2, 2, 4, 4, 2), ("ylo", "core", "z", "x", "yhi"))
    tok = P(("ylo", "core", "z", "x", "yhi"), None)
    weight = P(("z", "x", "yhi", "ylo", "core"), None)
    return jax.shard_map(
        per_device,
        mesh=fine,
        in_specs=(tok, P(("ylo", "core"), None), P(), P(), P(), P()) + (weight,) * 7,
        out_specs=tok,
        check_vma=False,
    )
```

time: 316 us -> 214 us (0.68)
  the two profiles are of different devices: /device:TPU:0 before, /device:TPU:68 now
where the time goes in v2:
time: 214 us
  Pallas kernels  211 us (99%)
  local copies, waits for them, and re-layouts  2.91 us (1%)
    pallas_call x1, Pallas kernels, per_device(): pl.pallas_call(kernel, out_shape=jax.ShapeDtypeStruct(tokens.shape, BF16)...  211 us

profile of v2, /device:TPU:68, one launch (start us, length us, event | category | flops | bytes accessed | tf_op | source)
XLA Modules:
  0.0 213.6 jit_solution(14016904913075916000)
XLA Ops:
  0.0 1.3 dynamic-slice_bitcast_fusion
  1.3 210.7 %shard_map.127 = bf16[40,2048]{1,0:T(8,128)(2,1)} custom-call(s32[1,8]{1,0:T(1,128)} %lengths.1, bf16[40,2048]{1,0:T(8,128)(2,1)} %tokens.1, f32[1,128]{1,0:T(1,128)} %get-tuple-element.6.query_gain, f32[1,128]{1,0:T(1,128)} %get-tuple-element.5.key_gain, f32[1,2048]{1,0:T(1,128)} %bitcast.6, f32[1,2048]{1,0:T(1,128)} %bitcast.7, f32[16,2048]{1,0:T(8,128)} %query_w.1, ...), custom_call_target="tpu_custom_call" | custom-call | tf_op jit(solution)/shard_map/pallas_call | solution.py:420
  212.0 1.6 copy.15

commit v3 on v2

v3 whole, which is shorter than its diff:
```python
import math

import jax
import jax.numpy as jnp
from jax import lax
from jax.experimental import pallas as pl
from jax.experimental.pallas import tpu as pltpu
from jax.sharding import Mesh, PartitionSpec as P

HEAD_DIM = 128
NORM_EPSILON = 1e-06
ROPE_BASE = 500000.0
SIDE = 4
PLANE = SIDE * SIDE
COLUMN = 8
MESH = pl.DeviceIdType.MESH
F32 = jnp.float32
BF16 = jnp.bfloat16
HIGHEST = lax.Precision.HIGHEST


def remote(src, dst, send_sem, recv_sem, device):
    return pltpu.make_async_remote_copy(
        src_ref=src,
        dst_ref=dst,
        send_sem=send_sem,
        recv_sem=recv_sem,
        device_id=device,
        device_id_type=MESH,
    )


def plane_device(place):
    return {"z": place // SIDE, "x": lax.rem(place, SIDE)}


def dot(a, b):
    return jnp.dot(a, b, preferred_element_type=F32)


def kernel(
    lengths,
    tokens,
    query_gain,
    key_gain,
    attn_gain,
    mlp_gain,
    query_w,
    key_w,
    value_w,
    output_w,
    gate_w,
    up_w,
    down_w,
    out,
    stage_qkv,
    stage_mlp,
    qkv_all,
    mlp_all,
    out_all,
    down_all,
    tok_all,
    hid_all,
    proj,
    sq_all,
    scales,
    kv,
    queries,
    cosines,
    sines,
    opening,
    part_a,
    part_b,
    got_a,
    got_b,
    pass_a,
    pass_b,
    last_a,
    last_b,
    act,
    total,
    s_qkv,
    r_qkv,
    s_mlp,
    r_mlp,
    s_sq,
    r_sq,
    s_tok,
    r_tok,
    s_hid,
    r_hid,
    s_one_a,
    r_one_a,
    s_two_a,
    r_two_a,
    s_one_b,
    r_one_b,
    s_two_b,
    r_two_b,
    c_send,
    c_recv,
    s_kv,
    r_kv,
):
    z, x = lax.axis_index("z"), lax.axis_index("x")
    yhi, ylo, core = lax.axis_index("yhi"), lax.axis_index("ylo"), lax.axis_index("core")
    me = z * SIDE + x
    y = yhi * 2 + ylo
    slot = y * 2 + core
    rows = tokens.shape[0]
    set_rows = rows * PLANE
    group_rows = rows * SIDE
    features = tokens.shape[1]
    wide = features // 2
    hidden_width = act.shape[1]

    def y_peer(step):
        other = lax.rem(y + step, SIDE)
        return other, {"yhi": other // 2, "ylo": lax.rem(other, 2)}

    sibling = {"core": 1 - core}
    partner = {"yhi": 1 - yhi}

    barrier = pltpu.get_barrier_semaphore()

    @pl.loop(1, PLANE)
    def _(i):
        pl.semaphore_signal(
            barrier, inc=1, device_id=plane_device(lax.rem(me + i, PLANE)), device_id_type=MESH
        )

    @pl.loop(1, SIDE)
    def _(i):
        pl.semaphore_signal(barrier, inc=1, device_id=y_peer(i)[1], device_id_type=MESH)

    pl.semaphore_signal(barrier, inc=1, device_id=sibling, device_id_type=MESH)

    for p in range(PLANE):
        cols = slice(p * HEAD_DIM, (p + 1) * HEAD_DIM)
        for k, w in enumerate((query_w, key_w, value_w)):
            stage_qkv[p, :, k * HEAD_DIM : (k + 1) * HEAD_DIM] = w[:, cols].astype(BF16)
    for h in range(2):
        tok_all[h, me] = tokens[:, h * wide : (h + 1) * wide]
    pl.semaphore_wait(barrier, PLANE - 1 + SIDE)

    def plane_copy(i, src, dst, send, recv):
        peer = lax.rem(me + i, PLANE)
        return remote(src(peer), dst(me), send.at[i], recv.at[me], plane_device(peer))

    def plane_start(src, dst, send, recv):
        @pl.loop(1, PLANE)
        def _(i):
            plane_copy(i, src, dst, send, recv).start()

    def plane_wait_send(src, dst, send, recv):
        @pl.loop(1, PLANE)
        def _(i):
            plane_copy(i, src, dst, send, recv).wait_send()

    def plane_wait_recv(dst, send, recv):
        @pl.loop(1, PLANE)
        def _(i):
            peer = lax.rem(me + PLANE - i, PLANE)
            remote(dst(peer), dst(peer), send.at[0], recv.at[peer], plane_device(peer)).wait_recv()

    def along(h, order, i):
        if h == order:
            return z * SIDE + lax.rem(x + i, SIDE)
        return lax.rem(z + i, SIDE) * SIDE + x

    def gather_copy(ref, send, recv, h, order, j, i):
        held = along(h, 0, SIDE - j) if order == 1 else me
        return remote(
            ref.at[h, held],
            ref.at[h, held],
            send.at[h, order, j, i],
            recv.at[h, held],
            plane_device(along(h, order, i)),
        )

    def gather_wait(ref, send, recv, h, held):
        remote(
            ref.at[h, held], ref.at[h, held], send.at[0, 0, 0, 0], recv.at[h, held], sibling
        ).wait_recv()

    def gather_start(ref, send, recv):
        for order in range(2):

            @pl.loop(1, SIDE)
            def _(i):
                for h in range(2):
                    gather_copy(ref, send, recv, h, order, 0, i).start()

    def gather_relay(ref, send, recv):
        @pl.loop(1, SIDE)
        def _(j):
            for h in range(2):
                gather_wait(ref, send, recv, h, along(h, 0, SIDE - j))

                @pl.loop(1, SIDE)
                def _(i):
                    gather_copy(ref, send, recv, h, 1, j, i).start()

    def gather_wait_group(ref, send, recv, group):
        @pl.when(group != z)
        def _():
            @pl.loop(0, SIDE)
            def _(b):
                gather_wait(ref, send, recv, 0, group * SIDE + b)

        @pl.loop(1, SIDE)
        def _(i):
            gather_wait(ref, send, recv, 1, group * SIDE + lax.rem(x + i, SIDE))

    def gather_wait_send(ref, send, recv):
        @pl.loop(1, SIDE)
        def _(i):
            for h in range(2):
                gather_copy(ref, send, recv, h, 0, 0, i).wait_send()

                @pl.loop(0, SIDE)
                def _(j):
                    gather_copy(ref, send, recv, h, 1, j, i).wait_send()

    def gathered(ref, group):
        halves = []
        for h in range(2):
            blocks = [ref[h, group * SIDE + b].astype(F32) for b in range(SIDE)]
            halves.append(jnp.concatenate(blocks, axis=0).astype(BF16))
        return jnp.concatenate(halves, axis=1)

    def sum_first(group, part, got, send, recv):
        def tall():
            return remote(
                part.at[0, pl.ds(group * SIDE, SIDE)],
                got.at[0, z],
                send.at[0, 0, group],
                recv.at[0, 0, z],
                {"z": group},
            )

        def flat(i):
            other = lax.rem(x + i, SIDE)
            return remote(
                part.at[1, group * SIDE + other],
                got.at[1, x, group],
                send.at[1, i, group],
                recv.at[1, x, group],
                {"x": other},
            )

        return tall, flat

    def sum_start(group, move):
        tall, flat = sum_first(group, *move)

        @pl.when(group != z)
        def _():
            tall().start()

        @pl.loop(1, SIDE)
        def _(i):
            flat(i).start()

    def sum_wait_send(move):
        @pl.loop(1, SIDE)
        def _(i):
            sum_first(lax.rem(z + i, SIDE), *move)[0]().wait_send()

        @pl.loop(0, SIDE)
        def _(group):
            @pl.loop(1, SIDE)
            def _(i):
                sum_first(group, *move)[1](i).wait_send()

    def second_copy(h, i, passed, last, send, recv):
        own = x if h == 0 else z
        other = lax.rem(own + i, SIDE)
        return remote(
            passed.at[h, other],
            last.at[h, own],
            send.at[h, i],
            recv.at[h, own],
            {"x": other} if h == 0 else {"z": other},
        )

    def sum_finish(move, second):
        part, got, send, recv = move
        passed, last, send_two, recv_two = second

        @pl.loop(1, SIDE)
        def _(i):
            other = lax.rem(z + i, SIDE)
            remote(
                got.at[0, other], got.at[0, other], send.at[0, 0, 0], recv.at[0, 0, other], sibling
            ).wait_recv()

        @pl.loop(1, SIDE + 1)
        def _(i):
            other = lax.rem(x + i, SIDE)
            acc = part[0, z * SIDE + other].astype(F32)
            for j in range(1, SIDE):
                acc = acc + got[0, lax.rem(z + j, SIDE), other].astype(F32)
            passed[0, other] = acc.astype(BF16)

            @pl.when(i < SIDE)
            def _():
                second_copy(0, i, *second).start()

        @pl.loop(1, SIDE + 1)
        def _(i):
            other = lax.rem(z + i, SIDE)

            @pl.loop(1, SIDE)
            def _(j):
                source = lax.rem(x + j, SIDE)
                remote(
                    got.at[1, source, other],
                    got.at[1, source, other],
                    send.at[0, 0, 0],
                    recv.at[1, source, other],
                    sibling,
                ).wait_recv()

            acc = part[1, other * SIDE + x].astype(F32)
            for j in range(1, SIDE):
                acc = acc + got[1, lax.rem(x + j, SIDE), other].astype(F32)
            passed[1, other] = acc.astype(BF16)

            @pl.when(i < SIDE)
            def _():
                second_copy(1, i, *second).start()

        for h in range(2):
            own = x if h == 0 else z

            @pl.loop(1, SIDE)
            def _(i):
                other = lax.rem(own + i, SIDE)
                remote(
                    last.at[h, other],
                    last.at[h, other],
                    send_two.at[h, 0],
                    recv_two.at[h, other],
                    sibling,
                ).wait_recv()

            acc = passed[h, own].astype(F32)
            for i in range(1, SIDE):
                acc = acc + last[h, lax.rem(own + i, SIDE)].astype(F32)
            total[:, h * wide : (h + 1) * wide] = acc

    def second_wait_send(second):
        @pl.loop(1, SIDE)
        def _(i):
            for h in range(2):
                second_copy(h, i, *second).wait_send()

    def normed(gain):
        values_in = total[...]
        mean = jnp.mean(values_in * values_in, axis=-1, keepdims=True)
        return values_in * lax.rsqrt(mean + NORM_EPSILON) * gain[...]

    def column_y(kind, view, i):
        other, device = y_peer(i)
        return remote(view(slot), view(slot), c_send.at[kind, i], c_recv.at[kind, slot], device)

    def column_core(kind, view, i):
        held = y_peer(i)[0] * 2 + core
        return remote(
            view(held), view(held), c_send.at[kind, SIDE + i], c_recv.at[kind, held], sibling
        )

    def column_start(kind, view):
        @pl.loop(1, SIDE)
        def _(i):
            column_y(kind, view, i).start()

        column_core(kind, view, 0).start()

    def column_wait(kind, view, held):
        remote(
            view(held), view(held), c_send.at[kind, 0], c_recv.at[kind, held], sibling
        ).wait_recv()

    def column_pass(kind, view):
        @pl.loop(1, SIDE)
        def _(i):
            column_wait(kind, view, y_peer(i)[0] * 2 + core)
            column_core(kind, view, i).start()

    def column_finish(kind, view):
        @pl.loop(0, SIDE)
        def _(i):
            column_wait(kind, view, y_peer(i)[0] * 2 + 1 - core)

    def column_wait_send(kind, view):
        @pl.loop(1, SIDE)
        def _(i):
            column_y(kind, view, i).wait_send()

        @pl.loop(0, SIDE)
        def _(i):
            column_core(kind, view, i).wait_send()

    column = (
        (0, lambda q: qkv_all.at[:, q]),
        (1, lambda q: out_all.at[q]),
        (2, lambda q: mlp_all.at[:, q]),
        (3, lambda q: down_all.at[q]),
    )
    qkv_move = (lambda p: stage_qkv.at[p], lambda p: qkv_all.at[p, slot], s_qkv, r_qkv)
    mlp_move = (lambda p: stage_mlp.at[p], lambda p: mlp_all.at[p, slot], s_mlp, r_mlp)
    sq_move = (lambda p: sq_all.at[me], lambda p: sq_all.at[p], s_sq, r_sq)
    tok_move = (tok_all, s_tok, r_tok)
    hid_move = (hid_all, s_hid, r_hid)
    one_a = (part_a, got_a, s_one_a, r_one_a)
    two_a = (pass_a, last_a, s_two_a, r_two_a)
    one_b = (part_b, got_b, s_one_b, r_one_b)
    two_b = (pass_b, last_b, s_two_b, r_two_b)

    plane_start(*qkv_move)
    gather_start(*tok_move)
    qkv_all[me, slot] = stage_qkv[me]
    out_all[slot] = output_w[...].astype(BF16)
    down_all[slot] = down_w[...].astype(BF16)

    def numbered(index, which):
        return index + ((index * 1639) >> 16) * rows + which * rows

    flat = lax.broadcasted_iota(jnp.int32, (set_rows, HEAD_DIM), 0)
    row = numbered(flat, yhi)
    start = jnp.zeros_like(row)
    end = jnp.int32(0)
    for r in range(lengths.shape[1]):
        end = end + lengths[0, r]
        start = start + jnp.where(row >= end, lengths[0, r], 0)
    opening[...] = start
    lane = lax.broadcasted_iota(jnp.int32, (1, HEAD_DIM), 1)
    half = HEAD_DIM // 2
    step = jnp.where(lane < half, lane, lane - half).astype(F32)
    frequency = jnp.exp(step * (-2.0 * math.log(ROPE_BASE) / HEAD_DIM))
    angle = (row - start).astype(F32) * frequency
    cosines[...] = jnp.cos(angle)
    sines[...] = jnp.sin(angle) * jnp.where(lane < half, -1.0, 1.0)
    plane_wait_recv(*qkv_move[1:])
    column_start(*column[0])
    column_start(*column[1])
    column_start(*column[3])
    gather_relay(*tok_move)
    for p in range(PLANE):
        cols = slice(p * hidden_width, (p + 1) * hidden_width)
        for k, w in enumerate((gate_w, up_w)):
            stage_mlp[p, :, k * hidden_width : (k + 1) * hidden_width] = w[:, cols].astype(BF16)
    column_pass(*column[0])
    column_finish(*column[0])

    def chunk(i):
        return pl.ds(pl.multiple_of(i * group_rows, group_rows), group_rows)

    def rotated(values_in, gain, here):
        scaled = values_in * gain
        return (scaled * cosines[here, :] + pltpu.roll(scaled, half, 1) * sines[here, :]).astype(
            BF16
        )

    @pl.loop(0, SIDE)
    def _(i):
        group = lax.rem(z + i, SIDE)
        here = chunk(group)
        gather_wait_group(*tok_move, group)
        made = dot(gathered(tok_all, group), qkv_all[...].reshape(features, 3 * HEAD_DIM))
        query, key = made[:, :HEAD_DIM], made[:, HEAD_DIM : 2 * HEAD_DIM]
        proj[here, :HEAD_DIM] = query * query
        proj[here, HEAD_DIM:] = key * key
        queries[here, :] = rotated(query, query_gain[...], here)
        kv[0, here, :HEAD_DIM] = rotated(key, key_gain[...], here)
        kv[0, here, HEAD_DIM:] = made[:, 2 * HEAD_DIM :].astype(BF16)

    pick = (
        lax.broadcasted_iota(jnp.int32, (8, 2 * HEAD_DIM), 1) // HEAD_DIM
        == lax.broadcasted_iota(jnp.int32, (8, 2 * HEAD_DIM), 0)
    ).astype(F32)
    sq_all[me] = lax.dot_general(
        pick, proj[...], (((1,), (1,)), ((), ())), precision=HIGHEST, preferred_element_type=F32
    )
    plane_start(*sq_move)
    kv_copy = remote(kv.at[0], kv.at[1], s_kv.at[0], r_kv.at[0], partner)
    kv_copy.start()
    plane_start(*mlp_move)
    mlp_all[me, slot] = stage_mlp[me]
    column_pass(*column[1])
    plane_wait_recv(*sq_move[1:])
    sums = sq_all[0]
    for p in range(1, PLANE):
        sums = sums + sq_all[p]
    scales[0] = lax.rsqrt(sums / features + NORM_EPSILON)
    scale_copy = remote(scales.at[0], scales.at[1], s_kv.at[1], r_kv.at[1], partner)
    scale_copy.start()
    query_scale = jnp.transpose(scales[0]) * (1.0 / math.sqrt(HEAD_DIM))
    proj[:, :8] = query_scale
    column_finish(*column[1])
    kv_copy.wait_recv()
    scale_copy.wait_recv()

    lane_index = lax.broadcasted_iota(jnp.int32, (1, set_rows), 1)

    @pl.loop(1, SIDE + 1)
    def _(i):
        group = lax.rem(z + i, SIDE)
        here = chunk(group)
        key_row = jnp.concatenate([numbered(lane_index, yhi), numbered(lane_index, 1 - yhi)], axis=1)
        key_scale = jnp.concatenate([scales[0, 1:2, :], scales[1, 1:2, :]], axis=1)
        own = lax.broadcasted_iota(jnp.int32, (group_rows, 1), 0) + group * group_rows
        own_row = numbered(own, yhi)
        first = opening[here, :][:, 0:1]
        scores = lax.dot_general(
            queries[here, :],
            kv[:, :, :HEAD_DIM].reshape(2 * set_rows, HEAD_DIM),
            (((1,), (1,)), ((), ())),
            preferred_element_type=F32,
        )
        scores = scores * proj[here, :HEAD_DIM][:, 0:1] * key_scale
        scores = jnp.where((key_row >= first) & (key_row <= own_row), scores, -1e30)
        weights = jnp.exp(scores - jnp.max(scores, axis=1, keepdims=True))
        weights = weights / jnp.sum(weights, axis=1, keepdims=True)
        attended = dot(
            weights.astype(BF16), kv[:, :, HEAD_DIM:].reshape(2 * set_rows, HEAD_DIM)
        ).astype(BF16)
        summed = dot(attended, out_all[...].reshape(HEAD_DIM, features))
        for b in range(SIDE):
            for h in range(2):
                part_a[h, group * SIDE + b] = summed[
                    b * rows : (b + 1) * rows, h * wide : (h + 1) * wide
                ].astype(BF16)
        sum_start(group, one_a)

    plane_wait_recv(*mlp_move[1:])
    column_start(*column[2])
    column_pass(*column[3])
    sum_finish(one_a, two_a)
    hidden = (tokens[...].astype(F32) + normed(attn_gain)).astype(BF16)
    for h in range(2):
        hid_all[h, me] = hidden[:, h * wide : (h + 1) * wide]
    gather_start(*hid_move)
    gather_relay(*hid_move)
    column_pass(*column[2])
    column_finish(*column[2])
    column_finish(*column[3])

    @pl.loop(0, SIDE)
    def _(i):
        group = lax.rem(z + i, SIDE)
        gather_wait_group(*hid_move, group)
        values_in = gathered(hid_all, group)
        tile = 256
        for c in range(hidden_width // tile):
            lo = c * tile
            gate = dot(values_in, mlp_all[:, :, :, lo : lo + tile].reshape(features, tile))
            lo = lo + hidden_width
            up = dot(values_in, mlp_all[:, :, :, lo : lo + tile].reshape(features, tile))
            act[:, c * tile : (c + 1) * tile] = (gate / (1.0 + jnp.exp(-gate)) * up).astype(BF16)
        across = 512
        for c in range(features // across):
            cols = slice(c * across, (c + 1) * across)
            summed = dot(act[...], down_all[:, :, cols].reshape(hidden_width, across))
            h, lo = c * across // wide, c * across % wide
            for b in range(SIDE):
                part_b[h, group * SIDE + b, :, lo : lo + across] = summed[
                    b * rows : (b + 1) * rows
                ].astype(BF16)
        sum_start(group, one_b)

    sum_finish(one_b, two_b)
    base = jnp.concatenate([hid_all[0, me], hid_all[1, me]], axis=1).astype(F32)
    out[...] = (base + normed(mlp_gain)).astype(BF16)

    for move in (qkv_move, mlp_move, sq_move):
        plane_wait_send(*move)
    for move in (tok_move, hid_move):
        gather_wait_send(*move)
    for one, two in ((one_a, two_a), (one_b, two_b)):
        sum_wait_send(one)
        second_wait_send(two)
    for kind, view in column:
        column_wait_send(kind, view)
    kv_copy.wait_send()
    scale_copy.wait_send()


def per_device(tokens, lengths, query_gain, key_gain, attn_gain, mlp_gain, *weights):
    place = lax.axis_index("z") * SIDE + lax.axis_index("x")
    q_part = lax.dynamic_slice_in_dim(query_gain, place * HEAD_DIM, HEAD_DIM)[None]
    k_part = lax.dynamic_slice_in_dim(key_gain, place * HEAD_DIM, HEAD_DIM)[None]
    rows, features = tokens.shape
    depth = weights[0].shape[0]
    ff = weights[4].shape[1] // PLANE
    down_depth = weights[6].shape[0]
    set_rows = rows * PLANE
    vmem = pl.BlockSpec(memory_space=pltpu.VMEM)
    dma = pltpu.SemaphoreType.DMA
    half = (rows, features // 2)
    return pl.pallas_call(
        kernel,
        out_shape=jax.ShapeDtypeStruct(tokens.shape, BF16),
        in_specs=[pl.BlockSpec(memory_space=pltpu.SMEM)] + [vmem] * 12,
        out_specs=vmem,
        scratch_shapes=[
            pltpu.VMEM((PLANE, depth, 3 * HEAD_DIM), BF16),
            pltpu.VMEM((PLANE, depth, 2 * ff), BF16),
            pltpu.VMEM((PLANE, COLUMN, depth, 3 * HEAD_DIM), BF16),
            pltpu.VMEM((PLANE, COLUMN, depth, 2 * ff), BF16),
            pltpu.VMEM((COLUMN, depth, features), BF16),
            pltpu.VMEM((COLUMN, down_depth, features), BF16),
            pltpu.VMEM((2, PLANE) + half, BF16),
            pltpu.VMEM((2, PLANE) + half, BF16),
            pltpu.VMEM((set_rows, 2 * HEAD_DIM), F32),
            pltpu.VMEM((PLANE, 8, set_rows), F32),
            pltpu.VMEM((2, 8, set_rows), F32),
            pltpu.VMEM((2, set_rows, 2 * HEAD_DIM), BF16),
            pltpu.VMEM((set_rows, HEAD_DIM), BF16),
            pltpu.VMEM((set_rows, HEAD_DIM), F32),
            pltpu.VMEM((set_rows, HEAD_DIM), F32),
            pltpu.VMEM((set_rows, HEAD_DIM), jnp.int32),
            pltpu.VMEM((2, PLANE) + half, BF16),
            pltpu.VMEM((2, PLANE) + half, BF16),
            pltpu.VMEM((2, SIDE, SIDE) + half, BF16),
            pltpu.VMEM((2, SIDE, SIDE) + half, BF16),
            pltpu.VMEM((2, SIDE) + half, BF16),
            pltpu.VMEM((2, SIDE) + half, BF16),
            pltpu.VMEM((2, SIDE) + half, BF16),
            pltpu.VMEM((2, SIDE) + half, BF16),
            pltpu.VMEM((rows * SIDE, ff), BF16),
            pltpu.VMEM((rows, features), F32),
        ]
        + [dma((PLANE,))] * 6
        + [dma((2, 2, SIDE, SIDE)), dma((2, PLANE))] * 2
        + [dma((2, SIDE, SIDE)), dma((2, SIDE, SIDE)), dma((2, SIDE)), dma((2, SIDE))] * 2
        + [dma((4, COLUMN)), dma((4, COLUMN)), dma((2,)), dma((2,))],
        compiler_params=pltpu.CompilerParams(
            collective_id=0, has_side_effects=True, vmem_limit_bytes=60 << 20
        ),
    )(lengths, tokens, q_part, k_part, attn_gain[None], mlp_gain[None], *weights)


def solution(mesh):
    fine = Mesh(mesh.devices.reshape(2, 2, 4, 4, 2), ("ylo", "core", "z", "x", "yhi"))
    tok = P(("ylo", "core", "z", "x", "yhi"), None)
    weight = P(("z", "x", "yhi", "ylo", "core"), None)
    return jax.shard_map(
        per_device,
        mesh=fine,
        in_specs=(tok, P(("ylo", "core"), None), P(), P(), P(), P()) + (weight,) * 7,
        out_specs=tok,
        check_vma=False,
    )
```

time: 214 us -> 123 us (0.57)
  the two profiles are of different devices: /device:TPU:68 before, /device:TPU:0 now
where the time goes in v3:
time: 123 us; the launch traced here: 122 us
  Pallas kernels  119 us (97%)
  local copies, waits for them, and re-layouts  2.91 us (2%)
    pallas_call x1, Pallas kernels, per_device(): pl.pallas_call(kernel, out_shape=jax.ShapeDtypeStruct(tokens.shape, BF16)...  119 us

profile of v3, /device:TPU:0, one launch (start us, length us, event | category | flops | bytes accessed | tf_op | source)
XLA Modules:
  0.0 122.1 jit_solution(13420550398800558325)
XLA Ops:
  0.0 1.3 %dynamic-slice_bitcast_fusion = (f32[1,128]{1,0:T(1,128)}, f32[1,128]{1,0:T(1,128)}) fusion(f32[2048]{0:T(1024)} %param.16, s32[]{:T(128)S(6)} %select_n.4, f32[2048]{0:T(1024)} %param.15), kind=kLoop, calls=%fused_computation | loop fusion | bytes 2052 | tf_op jit(solution)/shard_map/broadcast_in_dim | solution.py:594
  1.3 119.2 %shard_map.127 = bf16[40,2048]{1,0:T(8,128)(2,1)} custom-call(s32[1,8]{1,0:T(1,128)} %lengths.1, bf16[40,2048]{1,0:T(8,128)(2,1)} %tokens.1, f32[1,128]{1,0:T(1,128)} %get-tuple-element.6.query_gain, f32[1,128]{1,0:T(1,128)} %get-tuple-element.5.key_gain, f32[1,2048]{1,0:T(1,128)} %bitcast.6, f32[1,2048]{1,0:T(1,128)} %bitcast.7, f32[16,2048]{1,0:T(8,128)} %query_w.1, ...), custom_call_target="tpu_custom_call" | custom-call | tf_op jit(solution)/shard_map/pallas_call | solution.py:603
  120.5 1.6 %copy.15 = bf16[40,2048]{1,0:T(8,128)(2,1)} copy(bf16[40,2048]{1,0:T(8,128)(2,1)} %shard_map.127) | data formatting | bytes 327680

commit v4 on v3

--- a/solution.py
+++ b/solution.py
@@ -41,6 +41,18 @@
 def kernel(
     lengths,
     tokens,
+    query_gain_in,
+    key_gain_in,
+    attn_gain_in,
+    mlp_gain_in,
+    query_in,
+    key_in,
+    value_in,
+    output_in,
+    gate_in,
+    up_in,
+    down_in,
+    out,
     query_gain,
     key_gain,
     attn_gain,
@@ -52,7 +64,6 @@
     gate_w,
     up_w,
     down_w,
-    out,
     stage_qkv,
     stage_mlp,
     qkv_all,
@@ -64,6 +75,7 @@
     proj,
     sq_all,
     scales,
+    key_scale,
     kv,
     queries,
     cosines,
@@ -101,6 +113,9 @@
     c_recv,
     s_kv,
     r_kv,
+    s_scale,
+    r_scale,
+    fetch,
 ):
     z, x = lax.axis_index("z"), lax.axis_index("x")
     yhi, ylo, core = lax.axis_index("yhi"), lax.axis_index("ylo"), lax.axis_index("core")
@@ -135,12 +150,31 @@
 
     pl.semaphore_signal(barrier, inc=1, device_id=sibling, device_id_type=MESH)
 
+    inputs = [(tokens.at[:, pl.ds(h * wide, wide)], tok_all.at[h, me]) for h in range(2)] + [
+        (query_in, query_w),
+        (key_in, key_w),
+        (value_in, value_w),
+        (output_in, output_w),
+        (down_in, down_w),
+        (query_gain_in, query_gain),
+        (key_gain_in, key_gain),
+        (attn_gain_in, attn_gain),
+        (mlp_gain_in, mlp_gain),
+        (gate_in, gate_w),
+        (up_in, up_w),
+    ]
+    fetches = [pltpu.make_async_copy(*pair, fetch.at[i]) for i, pair in enumerate(inputs)]
+    for copy in fetches:
+        copy.start()
+
+    for copy in fetches[2:5]:
+        copy.wait()
     for p in range(PLANE):
         cols = slice(p * HEAD_DIM, (p + 1) * HEAD_DIM)
         for k, w in enumerate((query_w, key_w, value_w)):
             stage_qkv[p, :, k * HEAD_DIM : (k + 1) * HEAD_DIM] = w[:, cols].astype(BF16)
-    for h in range(2):
-        tok_all[h, me] = tokens[:, h * wide : (h + 1) * wide]
+    for copy in fetches[:2]:
+        copy.wait()
     pl.semaphore_wait(barrier, PLANE - 1 + SIDE)
 
     def plane_copy(i, src, dst, send, recv):
@@ -422,6 +456,8 @@
     plane_start(*qkv_move)
     gather_start(*tok_move)
     qkv_all[me, slot] = stage_qkv[me]
+    for copy in fetches[5:]:
+        copy.wait()
     out_all[slot] = output_w[...].astype(BF16)
     down_all[slot] = down_w[...].astype(BF16)
 
@@ -446,7 +482,6 @@
     plane_wait_recv(*qkv_move[1:])
     column_start(*column[0])
     column_start(*column[1])
-    column_start(*column[3])
     gather_relay(*tok_move)
     for p in range(PLANE):
         cols = slice(p * hidden_width, (p + 1) * hidden_width)
@@ -464,6 +499,14 @@
             BF16
         )
 
+    def kv_copy(group):
+        here = chunk(group)
+        return remote(
+            kv.at[0, here], kv.at[1, here], s_kv.at[group], r_kv.at[group], partner
+        )
+
+    sq_all[me] = jnp.zeros_like(sq_all[me])
+
     @pl.loop(0, SIDE)
     def _(i):
         group = lax.rem(z + i, SIDE)
@@ -471,22 +514,25 @@
         gather_wait_group(*tok_move, group)
         made = dot(gathered(tok_all, group), qkv_all[...].reshape(features, 3 * HEAD_DIM))
         query, key = made[:, :HEAD_DIM], made[:, HEAD_DIM : 2 * HEAD_DIM]
-        proj[here, :HEAD_DIM] = query * query
-        proj[here, HEAD_DIM:] = key * key
-        queries[here, :] = rotated(query, query_gain[...], here)
-        kv[0, here, :HEAD_DIM] = rotated(key, key_gain[...], here)
+        queries[here, :] = rotated(query, query_gain[pl.ds(me, 1), :], here)
+        kv[0, here, :HEAD_DIM] = rotated(key, key_gain[pl.ds(me, 1), :], here)
         kv[0, here, HEAD_DIM:] = made[:, 2 * HEAD_DIM :].astype(BF16)
-
-    pick = (
-        lax.broadcasted_iota(jnp.int32, (8, 2 * HEAD_DIM), 1) // HEAD_DIM
-        == lax.broadcasted_iota(jnp.int32, (8, 2 * HEAD_DIM), 0)
-    ).astype(F32)
-    sq_all[me] = lax.dot_general(
-        pick, proj[...], (((1,), (1,)), ((), ())), precision=HIGHEST, preferred_element_type=F32
-    )
+        kv_copy(group).start()
+        pick = (
+            lax.broadcasted_iota(jnp.int32, (8, 2 * HEAD_DIM), 1) // HEAD_DIM * SIDE + group
+            == lax.broadcasted_iota(jnp.int32, (8, 2 * HEAD_DIM), 0)
+        ).astype(F32)
+        both = made[:, : 2 * HEAD_DIM]
+        sq_all[me] += lax.dot_general(
+            pick,
+            both * both,
+            (((1,), (1,)), ((), ())),
+            precision=HIGHEST,
+            preferred_element_type=F32,
+        )
+
     plane_start(*sq_move)
-    kv_copy = remote(kv.at[0], kv.at[1], s_kv.at[0], r_kv.at[0], partner)
-    kv_copy.start()
+    column_start(*column[3])
     plane_start(*mlp_move)
     mlp_all[me, slot] = stage_mlp[me]
     column_pass(*column[1])
@@ -495,13 +541,20 @@
     for p in range(1, PLANE):
         sums = sums + sq_all[p]
     scales[0] = lax.rsqrt(sums / features + NORM_EPSILON)
-    scale_copy = remote(scales.at[0], scales.at[1], s_kv.at[1], r_kv.at[1], partner)
+    scale_copy = remote(scales.at[0], scales.at[1], s_scale, r_scale, partner)
     scale_copy.start()
-    query_scale = jnp.transpose(scales[0]) * (1.0 / math.sqrt(HEAD_DIM))
-    proj[:, :8] = query_scale
+    proj[:, :8] = jnp.transpose(scales[0]) * (1.0 / math.sqrt(HEAD_DIM))
     column_finish(*column[1])
-    kv_copy.wait_recv()
+
+    @pl.loop(0, SIDE)
+    def _(group):
+        kv_copy(group).wait_recv()
+
     scale_copy.wait_recv()
+    for k in range(2):
+        for g in range(SIDE):
+            lo = k * set_rows + g * group_rows
+            key_scale[:, lo : lo + group_rows] = scales[k, SIDE + g : SIDE + g + 1, :]
 
     lane_index = lax.broadcasted_iota(jnp.int32, (1, set_rows), 1)
 
@@ -510,7 +563,10 @@
         group = lax.rem(z + i, SIDE)
         here = chunk(group)
         key_row = jnp.concatenate([numbered(lane_index, yhi), numbered(lane_index, 1 - yhi)], axis=1)
-        key_scale = jnp.concatenate([scales[0, 1:2, :], scales[1, 1:2, :]], axis=1)
+        query_lane = lax.broadcasted_iota(jnp.int32, (group_rows, 8), 1)
+        query_scale = jnp.sum(
+            jnp.where(query_lane == group, proj[:, :8], 0.0), axis=1, keepdims=True
+        )
         own = lax.broadcasted_iota(jnp.int32, (group_rows, 1), 0) + group * group_rows
         own_row = numbered(own, yhi)
         first = opening[here, :][:, 0:1]
@@ -520,7 +576,7 @@
             (((1,), (1,)), ((), ())),
             preferred_element_type=F32,
         )
-        scores = scores * proj[here, :HEAD_DIM][:, 0:1] * key_scale
+        scores = scores * query_scale * key_scale[...]
         scores = jnp.where((key_row >= first) & (key_row <= own_row), scores, -1e30)
         weights = jnp.exp(scores - jnp.max(scores, axis=1, keepdims=True))
         weights = weights / jnp.sum(weights, axis=1, keepdims=True)
@@ -539,7 +595,8 @@
     column_start(*column[2])
     column_pass(*column[3])
     sum_finish(one_a, two_a)
-    hidden = (tokens[...].astype(F32) + normed(attn_gain)).astype(BF16)
+    base = jnp.concatenate([tok_all[0, me], tok_all[1, me]], axis=1).astype(F32)
+    hidden = (base + normed(attn_gain)).astype(BF16)
     for h in range(2):
         hid_all[h, me] = hidden[:, h * wide : (h + 1) * wide]
     gather_start(*hid_move)
@@ -584,28 +641,36 @@
         second_wait_send(two)
     for kind, view in column:
         column_wait_send(kind, view)
-    kv_copy.wait_send()
     scale_copy.wait_send()
 
+    @pl.loop(0, SIDE)
+    def _(group):
+        kv_copy(group).wait_send()
+
 
 def per_device(tokens, lengths, query_gain, key_gain, attn_gain, mlp_gain, *weights):
-    place = lax.axis_index("z") * SIDE + lax.axis_index("x")
-    q_part = lax.dynamic_slice_in_dim(query_gain, place * HEAD_DIM, HEAD_DIM)[None]
-    k_part = lax.dynamic_slice_in_dim(key_gain, place * HEAD_DIM, HEAD_DIM)[None]
     rows, features = tokens.shape
     depth = weights[0].shape[0]
     ff = weights[4].shape[1] // PLANE
     down_depth = weights[6].shape[0]
     set_rows = rows * PLANE
     vmem = pl.BlockSpec(memory_space=pltpu.VMEM)
+    anywhere = pl.BlockSpec(memory_space=pl.ANY)
     dma = pltpu.SemaphoreType.DMA
     half = (rows, features // 2)
     return pl.pallas_call(
         kernel,
         out_shape=jax.ShapeDtypeStruct(tokens.shape, BF16),
-        in_specs=[pl.BlockSpec(memory_space=pltpu.SMEM)] + [vmem] * 12,
+        in_specs=[pl.BlockSpec(memory_space=pltpu.SMEM)] + [anywhere] * 12,
         out_specs=vmem,
         scratch_shapes=[
+            pltpu.VMEM((PLANE, HEAD_DIM), F32),
+            pltpu.VMEM((PLANE, HEAD_DIM), F32),
+            pltpu.VMEM((1, features), F32),
+            pltpu.VMEM((1, features), F32),
+        ]
+        + [pltpu.VMEM(w.shape, F32) for w in weights]
+        + [
             pltpu.VMEM((PLANE, depth, 3 * HEAD_DIM), BF16),
             pltpu.VMEM((PLANE, depth, 2 * ff), BF16),
             pltpu.VMEM((PLANE, COLUMN, depth, 3 * HEAD_DIM), BF16),
@@ -614,9 +679,10 @@
             pltpu.VMEM((COLUMN, down_depth, features), BF16),
             pltpu.VMEM((2, PLANE) + half, BF16),
             pltpu.VMEM((2, PLANE) + half, BF16),
-            pltpu.VMEM((set_rows, 2 * HEAD_DIM), F32),
-            pltpu.VMEM((PLANE, 8, set_rows), F32),
-            pltpu.VMEM((2, 8, set_rows), F32),
+            pltpu.VMEM((rows * SIDE, HEAD_DIM), F32),
+            pltpu.VMEM((PLANE, 8, rows * SIDE), F32),
+            pltpu.VMEM((2, 8, rows * SIDE), F32),
+            pltpu.VMEM((1, 2 * set_rows), F32),
             pltpu.VMEM((2, set_rows, 2 * HEAD_DIM), BF16),
             pltpu.VMEM((set_rows, HEAD_DIM), BF16),
             pltpu.VMEM((set_rows, HEAD_DIM), F32),
@@ -636,11 +702,20 @@
         + [dma((PLANE,))] * 6
         + [dma((2, 2, SIDE, SIDE)), dma((2, PLANE))] * 2
         + [dma((2, SIDE, SIDE)), dma((2, SIDE, SIDE)), dma((2, SIDE)), dma((2, SIDE))] * 2
-        + [dma((4, COLUMN)), dma((4, COLUMN)), dma((2,)), dma((2,))],
+        + [dma((4, COLUMN)), dma((4, COLUMN)), dma((SIDE,)), dma((SIDE,))]
+        + [dma(()), dma(()), dma((16,))],
         compiler_params=pltpu.CompilerParams(
             collective_id=0, has_side_effects=True, vmem_limit_bytes=60 << 20
         ),
-    )(lengths, tokens, q_part, k_part, attn_gain[None], mlp_gain[None], *weights)
+    )(
+        lengths,
+        tokens,
+        query_gain.reshape(PLANE, HEAD_DIM),
+        key_gain.reshape(PLANE, HEAD_DIM),
+        attn_gain[None],
+        mlp_gain[None],
+        *weights,
+    )
 
 
 def solution(mesh):

time: 123 us -> 127 us (1.033)
  Pallas kernels: 119 us -> 125 us
  local copies, waits for them, and re-layouts: 2.91 us -> 1.59 us
    pallas_call x1, Pallas kernels: 119 us -> 125 us  [per_device(): pl.pallas_call(kernel, out_shape=jax.ShapeDtypeStruct(tokens.shape, BF16)...]
    broadcast_in_dim x1 -> x0, local copies, waits for them, and re-layouts: 1.31 us -> none  [per_device(): lax.dynamic_slice_in_dim(key_gain, place * HEAD_DIM, HEAD_DIM)[None]]
where the time goes in v4:
time: 127 us
  Pallas kernels  125 us (98%)
  local copies, waits for them, and re-layouts  1.59 us (1%)
    pallas_call x1, Pallas kernels, per_device(): pl.pallas_call(kernel, out_shape=jax.ShapeDtypeStruct(tokens.shape, BF16)...  125 us

profile of v4, /device:TPU:0, one launch (start us, length us, event | category | flops | bytes accessed | tf_op | source)
XLA Modules:
  0.0 126.7 jit_solution(15194533072816748135)
XLA Ops:
  0.0 125.1 %shard_map.127 = bf16[40,2048]{1,0:T(8,128)(2,1)} custom-call(s32[1,8]{1,0:T(1,128)} %lengths.1, bf16[40,2048]{1,0:T(8,128)(2,1)} %tokens.1, f32[16,128]{1,0:T(8,128)} %bitcast.4, f32[16,128]{1,0:T(8,128)} %bitcast.5, f32[1,2048]{1,0:T(1,128)} %bitcast.6, f32[1,2048]{1,0:T(1,128)} %bitcast.7, f32[16,2048]{1,0:T(8,128)} %query_in.1, f32[16,2048]{1,0:T(8,128)} %key_in.1, ...), custom_call_target="tpu_custom_call" | custom-call | tf_op jit(solution)/shard_map/pallas_call | solution.py:661
  125.1 1.6 %copy.15 = bf16[40,2048]{1,0:T(8,128)(2,1)} copy(bf16[40,2048]{1,0:T(8,128)(2,1)} %shard_map.127) | data formatting | bytes 327680

commit v5 on v4

--- a/solution.py
+++ b/solution.py
@@ -116,6 +116,7 @@
     s_scale,
     r_scale,
     fetch,
+    entered,
 ):
     z, x = lax.axis_index("z"), lax.axis_index("x")
     yhi, ylo, core = lax.axis_index("yhi"), lax.axis_index("ylo"), lax.axis_index("core")
@@ -138,15 +139,10 @@
 
     barrier = pltpu.get_barrier_semaphore()
 
-    @pl.loop(1, PLANE)
-    def _(i):
-        pl.semaphore_signal(
-            barrier, inc=1, device_id=plane_device(lax.rem(me + i, PLANE)), device_id_type=MESH
-        )
-
     @pl.loop(1, SIDE)
     def _(i):
-        pl.semaphore_signal(barrier, inc=1, device_id=y_peer(i)[1], device_id_type=MESH)
+        for device in ({"x": lax.rem(x + i, SIDE)}, {"z": lax.rem(z + i, SIDE)}, y_peer(i)[1]):
+            pl.semaphore_signal(barrier, inc=1, device_id=device, device_id_type=MESH)
 
     pl.semaphore_signal(barrier, inc=1, device_id=sibling, device_id_type=MESH)
 
@@ -175,7 +171,13 @@
             stage_qkv[p, :, k * HEAD_DIM : (k + 1) * HEAD_DIM] = w[:, cols].astype(BF16)
     for copy in fetches[:2]:
         copy.wait()
-    pl.semaphore_wait(barrier, PLANE - 1 + SIDE)
+    pl.semaphore_wait(barrier, 3 * (SIDE - 1) + 1)
+
+    @pl.loop(1, SIDE)
+    def _(i):
+        pl.semaphore_signal(
+            entered, inc=1, device_id={"x": lax.rem(x + i, SIDE)}, device_id_type=MESH
+        )
 
     def plane_copy(i, src, dst, send, recv):
         peer = lax.rem(me + i, PLANE)
@@ -322,27 +324,7 @@
         part, got, send, recv = move
         passed, last, send_two, recv_two = second
 
-        @pl.loop(1, SIDE)
-        def _(i):
-            other = lax.rem(z + i, SIDE)
-            remote(
-                got.at[0, other], got.at[0, other], send.at[0, 0, 0], recv.at[0, 0, other], sibling
-            ).wait_recv()
-
-        @pl.loop(1, SIDE + 1)
-        def _(i):
-            other = lax.rem(x + i, SIDE)
-            acc = part[0, z * SIDE + other].astype(F32)
-            for j in range(1, SIDE):
-                acc = acc + got[0, lax.rem(z + j, SIDE), other].astype(F32)
-            passed[0, other] = acc.astype(BF16)
-
-            @pl.when(i < SIDE)
-            def _():
-                second_copy(0, i, *second).start()
-
-        @pl.loop(1, SIDE + 1)
-        def _(i):
+        def across(i):
             other = lax.rem(z + i, SIDE)
 
             @pl.loop(1, SIDE)
@@ -361,9 +343,31 @@
                 acc = acc + got[1, lax.rem(x + j, SIDE), other].astype(F32)
             passed[1, other] = acc.astype(BF16)
 
+        @pl.loop(1, SIDE)
+        def _(i):
+            across(i)
+            second_copy(1, i, *second).start()
+
+        @pl.loop(1, SIDE)
+        def _(i):
+            other = lax.rem(z + i, SIDE)
+            remote(
+                got.at[0, other], got.at[0, other], send.at[0, 0, 0], recv.at[0, 0, other], sibling
+            ).wait_recv()
+
+        @pl.loop(1, SIDE + 1)
+        def _(i):
+            other = lax.rem(x + i, SIDE)
+            acc = part[0, z * SIDE + other].astype(F32)
+            for j in range(1, SIDE):
+                acc = acc + got[0, lax.rem(z + j, SIDE), other].astype(F32)
+            passed[0, other] = acc.astype(BF16)
+
             @pl.when(i < SIDE)
             def _():
-                second_copy(1, i, *second).start()
+                second_copy(0, i, *second).start()
+
+        across(SIDE)
 
         for h in range(2):
             own = x if h == 0 else z
@@ -453,8 +457,9 @@
     one_b = (part_b, got_b, s_one_b, r_one_b)
     two_b = (pass_b, last_b, s_two_b, r_two_b)
 
+    gather_start(*tok_move)
+    pl.semaphore_wait(entered, SIDE - 1)
     plane_start(*qkv_move)
-    gather_start(*tok_move)
     qkv_all[me, slot] = stage_qkv[me]
     for copy in fetches[5:]:
         copy.wait()
@@ -532,8 +537,6 @@
         )
 
     plane_start(*sq_move)
-    column_start(*column[3])
-    plane_start(*mlp_move)
     mlp_all[me, slot] = stage_mlp[me]
     column_pass(*column[1])
     plane_wait_recv(*sq_move[1:])
@@ -543,6 +546,7 @@
     scales[0] = lax.rsqrt(sums / features + NORM_EPSILON)
     scale_copy = remote(scales.at[0], scales.at[1], s_scale, r_scale, partner)
     scale_copy.start()
+    plane_start(*mlp_move)
     proj[:, :8] = jnp.transpose(scales[0]) * (1.0 / math.sqrt(HEAD_DIM))
     column_finish(*column[1])
 
@@ -555,6 +559,7 @@
         for g in range(SIDE):
             lo = k * set_rows + g * group_rows
             key_scale[:, lo : lo + group_rows] = scales[k, SIDE + g : SIDE + g + 1, :]
+    column_start(*column[3])
 
     lane_index = lax.broadcasted_iota(jnp.int32, (1, set_rows), 1)
 
@@ -703,7 +708,7 @@
         + [dma((2, 2, SIDE, SIDE)), dma((2, PLANE))] * 2
         + [dma((2, SIDE, SIDE)), dma((2, SIDE, SIDE)), dma((2, SIDE)), dma((2, SIDE))] * 2
         + [dma((4, COLUMN)), dma((4, COLUMN)), dma((SIDE,)), dma((SIDE,))]
-        + [dma(()), dma(()), dma((16,))],
+        + [dma(()), dma(()), dma((16,)), pltpu.SemaphoreType.REGULAR],
         compiler_params=pltpu.CompilerParams(
             collective_id=0, has_side_effects=True, vmem_limit_bytes=60 << 20
         ),

time: 127 us -> 123 us (0.969)
  Pallas kernels: 125 us -> 121 us
    pallas_call x1, Pallas kernels: 125 us -> 121 us  [per_device(): pl.pallas_call(kernel, out_shape=jax.ShapeDtypeStruct(tokens.shape, BF16)...]
where the time goes in v5:
time: 123 us
  Pallas kernels  121 us (98%)
  local copies, waits for them, and re-layouts  1.59 us (1%)
    pallas_call x1, Pallas kernels, per_device(): pl.pallas_call(kernel, out_shape=jax.ShapeDtypeStruct(tokens.shape, BF16)...  121 us

profile of v5, /device:TPU:0, one launch (start us, length us, event | category | flops | bytes accessed | tf_op | source)
XLA Modules:
  0.0 122.6 jit_solution(7767682037313142644)
XLA Ops:
  0.0 121.0 %shard_map.127 = bf16[40,2048]{1,0:T(8,128)(2,1)} custom-call(s32[1,8]{1,0:T(1,128)} %lengths.1, bf16[40,2048]{1,0:T(8,128)(2,1)} %tokens.1, f32[16,128]{1,0:T(8,128)} %bitcast.4, f32[16,128]{1,0:T(8,128)} %bitcast.5, f32[1,2048]{1,0:T(1,128)} %bitcast.6, f32[1,2048]{1,0:T(1,128)} %bitcast.7, f32[16,2048]{1,0:T(8,128)} %query_in.1, f32[16,2048]{1,0:T(8,128)} %key_in.1, ...), custom_call_target="tpu_custom_call" | custom-call | tf_op jit(solution)/shard_map/pallas_call | solution.py:666
  121.0 1.6 %copy.15 = bf16[40,2048]{1,0:T(8,128)(2,1)} copy(bf16[40,2048]{1,0:T(8,128)(2,1)} %shard_map.127) | data formatting | bytes 327680

commit v6 on v4

--- a/solution.py
+++ b/solution.py
@@ -218,22 +218,23 @@
         ).wait_recv()
 
     def gather_start(ref, send, recv):
-        for order in range(2):
-
-            @pl.loop(1, SIDE)
-            def _(i):
-                for h in range(2):
-                    gather_copy(ref, send, recv, h, order, 0, i).start()
+        for i in (1, 3, 2):
+            for h in range(2):
+                gather_copy(ref, send, recv, h, 0, 0, i).start()
+        for i in (1, 3, 2):
+            for h in range(2):
+                if (h, i) != (0, 2):
+                    gather_copy(ref, send, recv, h, 1, 0, i).start()
 
     def gather_relay(ref, send, recv):
-        @pl.loop(1, SIDE)
-        def _(j):
+        for j in (1, 3, 2):
             for h in range(2):
                 gather_wait(ref, send, recv, h, along(h, 0, SIDE - j))
-
-                @pl.loop(1, SIDE)
-                def _(i):
-                    gather_copy(ref, send, recv, h, 1, j, i).start()
+                for i in (1, 3, 2):
+                    if (h, i) != (0, 2):
+                        gather_copy(ref, send, recv, h, 1, j, i).start()
+        for j in (0, 1, 3, 2):
+            gather_copy(ref, send, recv, 0, 1, j, 2).start()
 
     def gather_wait_group(ref, send, recv, group):
         @pl.when(group != z)
@@ -255,6 +256,9 @@
                 @pl.loop(0, SIDE)
                 def _(j):
                     gather_copy(ref, send, recv, h, 1, j, i).wait_send()
+
+    def near_first(i):
+        return lax.rem(z + i + i // 2 * (1 - 2 * lax.rem(i, 2)), SIDE)
 
     def gathered(ref, group):
         halves = []
@@ -509,7 +513,7 @@
 
     @pl.loop(0, SIDE)
     def _(i):
-        group = lax.rem(z + i, SIDE)
+        group = near_first(i)
         here = chunk(group)
         gather_wait_group(*tok_move, group)
         made = dot(gathered(tok_all, group), qkv_all[...].reshape(features, 3 * HEAD_DIM))
@@ -532,8 +536,6 @@
         )
 
     plane_start(*sq_move)
-    column_start(*column[3])
-    plane_start(*mlp_move)
     mlp_all[me, slot] = stage_mlp[me]
     column_pass(*column[1])
     plane_wait_recv(*sq_move[1:])
@@ -543,6 +545,7 @@
     scales[0] = lax.rsqrt(sums / features + NORM_EPSILON)
     scale_copy = remote(scales.at[0], scales.at[1], s_scale, r_scale, partner)
     scale_copy.start()
+    plane_start(*mlp_move)
     proj[:, :8] = jnp.transpose(scales[0]) * (1.0 / math.sqrt(HEAD_DIM))
     column_finish(*column[1])
 
@@ -555,6 +558,7 @@
         for g in range(SIDE):
             lo = k * set_rows + g * group_rows
             key_scale[:, lo : lo + group_rows] = scales[k, SIDE + g : SIDE + g + 1, :]
+    column_start(*column[3])
 
     lane_index = lax.broadcasted_iota(jnp.int32, (1, set_rows), 1)
 
@@ -607,7 +611,7 @@
 
     @pl.loop(0, SIDE)
     def _(i):
-        group = lax.rem(z + i, SIDE)
+        group = near_first(i)
         gather_wait_group(*hid_move, group)
         values_in = gathered(hid_all, group)
         tile = 256

time: 127 us -> 115 us (0.906)
  the two profiles are of different devices: /device:TPU:0 before, /device:TPU:16 now
where the time goes in v6:
time: 115 us
  Pallas kernels  114 us (99%)
  local copies, waits for them, and re-layouts  1.59 us (1%)
    pallas_call x1, Pallas kernels, per_device(): pl.pallas_call(kernel, out_shape=jax.ShapeDtypeStruct(tokens.shape, BF16)...  114 us

profile of v6, /device:TPU:16, one launch (start us, length us, event | category | flops | bytes accessed | tf_op | source)
XLA Modules:
  0.0 115.2 jit_solution(6176322899721146138)
XLA Ops:
  0.0 113.6 %shard_map.127 = bf16[40,2048]{1,0:T(8,128)(2,1)} custom-call(s32[1,8]{1,0:T(1,128)} %lengths.1, bf16[40,2048]{1,0:T(8,128)(2,1)} %tokens.1, f32[16,128]{1,0:T(8,128)} %bitcast.4, f32[16,128]{1,0:T(8,128)} %bitcast.5, f32[1,2048]{1,0:T(1,128)} %bitcast.6, f32[1,2048]{1,0:T(1,128)} %bitcast.7, f32[16,2048]{1,0:T(8,128)} %query_in.1, f32[16,2048]{1,0:T(8,128)} %key_in.1, ...), custom_call_target="tpu_custom_call" | custom-call | tf_op jit(solution)/shard_map/pallas_call | solution.py:665
  113.6 1.6 %copy.15 = bf16[40,2048]{1,0:T(8,128)(2,1)} copy(bf16[40,2048]{1,0:T(8,128)(2,1)} %shard_map.127) | data formatting | bytes 327680

commit v7 on v6

--- a/solution.py
+++ b/solution.py
@@ -322,31 +322,11 @@
             {"x": other} if h == 0 else {"z": other},
         )
 
-    def sum_finish(move, second):
+    def sum_finish(move, second, order):
         part, got, send, recv = move
         passed, last, send_two, recv_two = second
 
-        @pl.loop(1, SIDE)
-        def _(i):
-            other = lax.rem(z + i, SIDE)
-            remote(
-                got.at[0, other], got.at[0, other], send.at[0, 0, 0], recv.at[0, 0, other], sibling
-            ).wait_recv()
-
-        @pl.loop(1, SIDE + 1)
-        def _(i):
-            other = lax.rem(x + i, SIDE)
-            acc = part[0, z * SIDE + other].astype(F32)
-            for j in range(1, SIDE):
-                acc = acc + got[0, lax.rem(z + j, SIDE), other].astype(F32)
-            passed[0, other] = acc.astype(BF16)
-
-            @pl.when(i < SIDE)
-            def _():
-                second_copy(0, i, *second).start()
-
-        @pl.loop(1, SIDE + 1)
-        def _(i):
+        def across(i):
             other = lax.rem(z + i, SIDE)
 
             @pl.loop(1, SIDE)
@@ -364,10 +344,33 @@
             for j in range(1, SIDE):
                 acc = acc + got[1, lax.rem(x + j, SIDE), other].astype(F32)
             passed[1, other] = acc.astype(BF16)
+            if i:
+                second_copy(1, i, *second).start()
+
+        for i in order[:2]:
+            across(i)
+
+        @pl.loop(1, SIDE)
+        def _(i):
+            other = lax.rem(z + i, SIDE)
+            remote(
+                got.at[0, other], got.at[0, other], send.at[0, 0, 0], recv.at[0, 0, other], sibling
+            ).wait_recv()
+
+        @pl.loop(1, SIDE + 1)
+        def _(i):
+            other = lax.rem(x + i, SIDE)
+            acc = part[0, z * SIDE + other].astype(F32)
+            for j in range(1, SIDE):
+                acc = acc + got[0, lax.rem(z + j, SIDE), other].astype(F32)
+            passed[0, other] = acc.astype(BF16)
 
             @pl.when(i < SIDE)
             def _():
-                second_copy(1, i, *second).start()
+                second_copy(0, i, *second).start()
+
+        for i in order[2:]:
+            across(i)
 
         for h in range(2):
             own = x if h == 0 else z
@@ -485,13 +488,13 @@
     sines[...] = jnp.sin(angle) * jnp.where(lane < half, -1.0, 1.0)
     plane_wait_recv(*qkv_move[1:])
     column_start(*column[0])
-    column_start(*column[1])
     gather_relay(*tok_move)
     for p in range(PLANE):
         cols = slice(p * hidden_width, (p + 1) * hidden_width)
         for k, w in enumerate((gate_w, up_w)):
             stage_mlp[p, :, k * hidden_width : (k + 1) * hidden_width] = w[:, cols].astype(BF16)
     column_pass(*column[0])
+    column_start(*column[1])
     column_finish(*column[0])
 
     def chunk(i):
@@ -536,6 +539,7 @@
         )
 
     plane_start(*sq_move)
+    plane_start(*mlp_move)
     mlp_all[me, slot] = stage_mlp[me]
     column_pass(*column[1])
     plane_wait_recv(*sq_move[1:])
@@ -545,7 +549,6 @@
     scales[0] = lax.rsqrt(sums / features + NORM_EPSILON)
     scale_copy = remote(scales.at[0], scales.at[1], s_scale, r_scale, partner)
     scale_copy.start()
-    plane_start(*mlp_move)
     proj[:, :8] = jnp.transpose(scales[0]) * (1.0 / math.sqrt(HEAD_DIM))
     column_finish(*column[1])
 
@@ -558,7 +561,8 @@
         for g in range(SIDE):
             lo = k * set_rows + g * group_rows
             key_scale[:, lo : lo + group_rows] = scales[k, SIDE + g : SIDE + g + 1, :]
-    column_start(*column[3])
+    plane_wait_recv(*mlp_move[1:])
+    column_start(*column[2])
 
     lane_index = lax.broadcasted_iota(jnp.int32, (1, set_rows), 1)
 
@@ -595,10 +599,8 @@
                 ].astype(BF16)
         sum_start(group, one_a)
 
-    plane_wait_recv(*mlp_move[1:])
-    column_start(*column[2])
-    column_pass(*column[3])
-    sum_finish(one_a, two_a)
+    column_start(*column[3])
+    sum_finish(one_a, two_a, (1, 2, 3, 0))
     base = jnp.concatenate([tok_all[0, me], tok_all[1, me]], axis=1).astype(F32)
     hidden = (base + normed(attn_gain)).astype(BF16)
     for h in range(2):
@@ -606,6 +608,7 @@
     gather_start(*hid_move)
     gather_relay(*hid_move)
     column_pass(*column[2])
+    column_pass(*column[3])
     column_finish(*column[2])
     column_finish(*column[3])
 
@@ -632,17 +635,8 @@
                 ].astype(BF16)
         sum_start(group, one_b)
 
-    sum_finish(one_b, two_b)
-    base = jnp.concatenate([hid_all[0, me], hid_all[1, me]], axis=1).astype(F32)
-    out[...] = (base + normed(mlp_gain)).astype(BF16)
-
     for move in (qkv_move, mlp_move, sq_move):
         plane_wait_send(*move)
-    for move in (tok_move, hid_move):
-        gather_wait_send(*move)
-    for one, two in ((one_a, two_a), (one_b, two_b)):
-        sum_wait_send(one)
-        second_wait_send(two)
     for kind, view in column:
         column_wait_send(kind, view)
     scale_copy.wait_send()
@@ -650,6 +644,17 @@
     @pl.loop(0, SIDE)
     def _(group):
         kv_copy(group).wait_send()
+
+    gather_wait_send(*tok_move)
+    sum_wait_send(one_a)
+    second_wait_send(two_a)
+    gather_wait_send(*hid_move)
+    sum_finish(one_b, two_b, (1, 3, 2, 0))
+    base = jnp.concatenate([hid_all[0, me], hid_all[1, me]], axis=1).astype(F32)
+    out[...] = (base + normed(mlp_gain)).astype(BF16)
+
+    sum_wait_send(one_b)
+    second_wait_send(two_b)
 
 
 def per_device(tokens, lengths, query_gain, key_gain, attn_gain, mlp_gain, *weights):

time: 115 us -> 111 us (0.965)
  the two profiles are of different devices: /device:TPU:16 before, /device:TPU:0 now
where the time goes in v7:
time: 111 us; the launch traced here: 110 us
  Pallas kernels  109 us (98%)
  local copies, waits for them, and re-layouts  1.59 us (1%)
    pallas_call x1, Pallas kernels, per_device(): pl.pallas_call(kernel, out_shape=jax.ShapeDtypeStruct(tokens.shape, BF16)...  109 us

profile of v7, /device:TPU:0, one launch (start us, length us, event | category | flops | bytes accessed | tf_op | source)
XLA Modules:
  0.0 110.4 jit_solution(1808295593779604754)
XLA Ops:
  0.0 108.8 %shard_map.127 = bf16[40,2048]{1,0:T(8,128)(2,1)} custom-call(s32[1,8]{1,0:T(1,128)} %lengths.1, bf16[40,2048]{1,0:T(8,128)(2,1)} %tokens.1, f32[16,128]{1,0:T(8,128)} %bitcast.4, f32[16,128]{1,0:T(8,128)} %bitcast.5, f32[1,2048]{1,0:T(1,128)} %bitcast.6, f32[1,2048]{1,0:T(1,128)} %bitcast.7, f32[16,2048]{1,0:T(8,128)} %query_in.1, f32[16,2048]{1,0:T(8,128)} %key_in.1, ...), custom_call_target="tpu_custom_call" | custom-call | tf_op jit(solution)/shard_map/pallas_call | solution.py:670
  108.8 1.6 %copy.15 = bf16[40,2048]{1,0:T(8,128)(2,1)} copy(bf16[40,2048]{1,0:T(8,128)(2,1)} %shard_map.127) | data formatting | bytes 327680

commit v8 on v7

--- a/solution.py
+++ b/solution.py
@@ -116,6 +116,8 @@
     s_scale,
     r_scale,
     fetch,
+    h_send,
+    h_recv,
 ):
     z, x = lax.axis_index("z"), lax.axis_index("x")
     yhi, ylo, core = lax.axis_index("yhi"), lax.axis_index("ylo"), lax.axis_index("core")
@@ -442,6 +444,43 @@
 
         @pl.loop(0, SIDE)
         def _(i):
+            column_core(kind, view, i).wait_send()
+
+    def half_view(k, held, e):
+        if k == 0:
+            return mlp_all.at[pl.ds(e * PLANE // 2, PLANE // 2), held]
+        depth = down_all.shape[1] // 2
+        return down_all.at[held, pl.ds(e * depth, depth)]
+
+    SIDES = ((SIDE - 1, 0, 1), (1, 1, SIDE - 1))
+
+    def half_copy(k, held, e, to):
+        piece = half_view(k, held, e)
+        return remote(piece, piece, h_send.at[k, e], h_recv.at[k, e], y_peer(to)[1])
+
+    def column_near(kind, view):
+        for i in (1, SIDE - 1):
+            column_y(kind, view, i).start()
+        column_core(kind, view, 0).start()
+
+    def column_relay(kind, view):
+        for off, e, to in SIDES:
+            held = y_peer(off)[0] * 2 + core
+            column_wait(kind, view, held)
+            half_copy(kind - 2, held, e, to).start()
+            column_core(kind, view, off).start()
+
+    def column_far(kind, view):
+        held = y_peer(2)[0] * 2 + core
+        for _, e, to in SIDES:
+            half_copy(kind - 2, held, e, to).wait_recv()
+        column_core(kind, view, 2).start()
+
+    def column_near_wait_send(kind, view):
+        for off, e, to in SIDES:
+            column_y(kind, view, off).wait_send()
+            half_copy(kind - 2, y_peer(off)[0] * 2 + core, e, to).wait_send()
+        for i in range(SIDE):
             column_core(kind, view, i).wait_send()
 
     column = (
@@ -561,8 +600,7 @@
         for g in range(SIDE):
             lo = k * set_rows + g * group_rows
             key_scale[:, lo : lo + group_rows] = scales[k, SIDE + g : SIDE + g + 1, :]
-    plane_wait_recv(*mlp_move[1:])
-    column_start(*column[2])
+    column_near(*column[3])
 
     lane_index = lax.broadcasted_iota(jnp.int32, (1, set_rows), 1)
 
@@ -599,16 +637,19 @@
                 ].astype(BF16)
         sum_start(group, one_a)
 
-    column_start(*column[3])
+    plane_wait_recv(*mlp_move[1:])
+    column_near(*column[2])
     sum_finish(one_a, two_a, (1, 2, 3, 0))
     base = jnp.concatenate([tok_all[0, me], tok_all[1, me]], axis=1).astype(F32)
     hidden = (base + normed(attn_gain)).astype(BF16)
     for h in range(2):
         hid_all[h, me] = hidden[:, h * wide : (h + 1) * wide]
     gather_start(*hid_move)
+    column_relay(*column[2])
+    column_relay(*column[3])
     gather_relay(*hid_move)
-    column_pass(*column[2])
-    column_pass(*column[3])
+    column_far(*column[2])
+    column_far(*column[3])
     column_finish(*column[2])
     column_finish(*column[3])
 
@@ -637,8 +678,10 @@
 
     for move in (qkv_move, mlp_move, sq_move):
         plane_wait_send(*move)
-    for kind, view in column:
+    for kind, view in column[:2]:
         column_wait_send(kind, view)
+    for kind, view in column[2:]:
+        column_near_wait_send(kind, view)
     scale_copy.wait_send()
 
     @pl.loop(0, SIDE)
@@ -712,7 +755,7 @@
         + [dma((2, 2, SIDE, SIDE)), dma((2, PLANE))] * 2
         + [dma((2, SIDE, SIDE)), dma((2, SIDE, SIDE)), dma((2, SIDE)), dma((2, SIDE))] * 2
         + [dma((4, COLUMN)), dma((4, COLUMN)), dma((SIDE,)), dma((SIDE,))]
-        + [dma(()), dma(()), dma((16,))],
+        + [dma(()), dma(()), dma((16,)), dma((2, 2)), dma((2, 2))],
         compiler_params=pltpu.CompilerParams(
             collective_id=0, has_side_effects=True, vmem_limit_bytes=60 << 20
         ),

time: 111 us -> 110 us (level)
  no operation moved by 1% of the time
where the time goes in v8:
time: 110 us
  Pallas kernels  109 us (99%)
  local copies, waits for them, and re-layouts  1.59 us (1%)
    pallas_call x1, Pallas kernels, per_device(): pl.pallas_call(kernel, out_shape=jax.ShapeDtypeStruct(tokens.shape, BF16)...  109 us

profile of v8, /device:TPU:0, one launch (start us, length us, event | category | flops | bytes accessed | tf_op | source)
XLA Modules:
  0.0 110.3 jit_solution(6867956604386040022)
XLA Ops:
  0.0 108.7 %shard_map.127 = bf16[40,2048]{1,0:T(8,128)(2,1)} custom-call(s32[1,8]{1,0:T(1,128)} %lengths.1, bf16[40,2048]{1,0:T(8,128)(2,1)} %tokens.1, f32[16,128]{1,0:T(8,128)} %bitcast.4, f32[16,128]{1,0:T(8,128)} %bitcast.5, f32[1,2048]{1,0:T(1,128)} %bitcast.6, f32[1,2048]{1,0:T(1,128)} %bitcast.7, f32[16,2048]{1,0:T(8,128)} %query_in.1, f32[16,2048]{1,0:T(8,128)} %key_in.1, ...), custom_call_target="tpu_custom_call" | custom-call | tf_op jit(solution)/shard_map/pallas_call | solution.py:713
  108.7 1.6 %copy.15 = bf16[40,2048]{1,0:T(8,128)(2,1)} copy(bf16[40,2048]{1,0:T(8,128)(2,1)} %shard_map.127) | data formatting | bytes 327680

commit v9 on v8

--- a/solution.py
+++ b/solution.py
@@ -291,16 +291,15 @@
 
         return tall, flat
 
-    def sum_start(group, move):
-        tall, flat = sum_first(group, *move)
-
+    def sum_start_tall(group, move):
         @pl.when(group != z)
         def _():
-            tall().start()
-
-        @pl.loop(1, SIDE)
-        def _(i):
-            flat(i).start()
+            sum_first(group, *move)[0]().start()
+
+    def sum_start_flat(group, move):
+        @pl.loop(1, SIDE)
+        def _(i):
+            sum_first(group, *move)[1](i).start()
 
     def sum_wait_send(move):
         @pl.loop(1, SIDE)
@@ -373,6 +372,8 @@
 
         for i in order[2:]:
             across(i)
+
+        sum_wait_send(move)
 
         for h in range(2):
             own = x if h == 0 else z
@@ -635,7 +636,8 @@
                 part_a[h, group * SIDE + b] = summed[
                     b * rows : (b + 1) * rows, h * wide : (h + 1) * wide
                 ].astype(BF16)
-        sum_start(group, one_a)
+        sum_start_tall(group, one_a)
+        sum_start_flat(group, one_a)
 
     plane_wait_recv(*mlp_move[1:])
     column_near(*column[2])
@@ -645,8 +647,8 @@
     for h in range(2):
         hid_all[h, me] = hidden[:, h * wide : (h + 1) * wide]
     gather_start(*hid_move)
+    column_relay(*column[3])
     column_relay(*column[2])
-    column_relay(*column[3])
     gather_relay(*hid_move)
     column_far(*column[2])
     column_far(*column[3])
@@ -655,7 +657,7 @@
 
     @pl.loop(0, SIDE)
     def _(i):
-        group = near_first(i)
+        group = near_first(lax.rem(i + 1, SIDE))
         gather_wait_group(*hid_move, group)
         values_in = gathered(hid_all, group)
         tile = 256
@@ -674,7 +676,9 @@
                 part_b[h, group * SIDE + b, :, lo : lo + across] = summed[
                     b * rows : (b + 1) * rows
                 ].astype(BF16)
-        sum_start(group, one_b)
+            if h == 0 and lo + across == wide:
+                sum_start_tall(group, one_b)
+        sum_start_flat(group, one_b)
 
     for move in (qkv_move, mlp_move, sq_move):
         plane_wait_send(*move)
@@ -689,14 +693,12 @@
         kv_copy(group).wait_send()
 
     gather_wait_send(*tok_move)
-    sum_wait_send(one_a)
     second_wait_send(two_a)
     gather_wait_send(*hid_move)
     sum_finish(one_b, two_b, (1, 3, 2, 0))
     base = jnp.concatenate([hid_all[0, me], hid_all[1, me]], axis=1).astype(F32)
     out[...] = (base + normed(mlp_gain)).astype(BF16)
 
-    sum_wait_send(one_b)
     second_wait_send(two_b)
 
 

time: 110 us -> 110 us (level)
  no operation moved by 1% of the time
where the time goes in v9:
time: 110 us
  Pallas kernels  109 us (99%)
  local copies, waits for them, and re-layouts  1.59 us (1%)
    pallas_call x1, Pallas kernels, per_device(): pl.pallas_call(kernel, out_shape=jax.ShapeDtypeStruct(tokens.shape, BF16)...  109 us

profile of v9, /device:TPU:0, one launch (start us, length us, event | category | flops | bytes accessed | tf_op | source)
XLA Modules:
  0.0 110.1 jit_solution(3260444751515286531)
XLA Ops:
  0.0 108.5 %shard_map.127 = bf16[40,2048]{1,0:T(8,128)(2,1)} custom-call(s32[1,8]{1,0:T(1,128)} %lengths.1, bf16[40,2048]{1,0:T(8,128)(2,1)} %tokens.1, f32[16,128]{1,0:T(8,128)} %bitcast.4, f32[16,128]{1,0:T(8,128)} %bitcast.5, f32[1,2048]{1,0:T(1,128)} %bitcast.6, f32[1,2048]{1,0:T(1,128)} %bitcast.7, f32[16,2048]{1,0:T(8,128)} %query_in.1, f32[16,2048]{1,0:T(8,128)} %key_in.1, ...), custom_call_target="tpu_custom_call" | custom-call | tf_op jit(solution)/shard_map/pallas_call | solution.py:715
  108.5 1.6 %copy.15 = bf16[40,2048]{1,0:T(8,128)(2,1)} copy(bf16[40,2048]{1,0:T(8,128)(2,1)} %shard_map.127) | data formatting | bytes 327680
